TPU v7x, 32 devices: a whole 2x2x4 slice. The times are simulated.
32 devices in a mesh: owner: 4 (over z), tok: 4 (over y, x), rep: 2 (over core).
Axes of the slice: x: 2, y: 2, z: 4, core: 2. Of those that a mesh axis runs over, the one named last changes fastest.
Arguments:
- tokens: bfloat16 [8192, 4096], P(('owner', 'rep'), 'tok'), may hold values from -6 to 6
- frozen_weight: bfloat16 [4096, 4096], P('tok'), may hold values from -0.09375 to 0.09375
- adapter_down: bfloat16 [400, 64, 4096], P('owner', None, 'tok'), may hold values from -0.09375 to 0.09375
- adapter_up: bfloat16 [400, 64, 4096], P('owner', None, 'tok'), may hold values from -0.75 to 0.75
- cotangent: bfloat16 [8192, 4096], P(('owner', 'rep'), 'tok'), may hold values from -6 to 6
- family_ids: int32 [64], replicated, may hold values from 0 to 399, as said below
Outputs:
- projected: bfloat16 [8192, 4096], P(('owner', 'rep'), 'tok')
- grad_input: bfloat16 [8192, 4096], P(('owner', 'rep'), 'tok')
- grad_down: float32 [400, 64, 4096], P('owner', 'rep', 'tok')
- grad_up: float32 [400, 64, 4096], P('owner', 'rep', 'tok')
Inputs may be any that keep to these rules, and one draw needn't show every extreme that they name: `family_ids`: block b is held by owner index b // (8 * 2) and rep index (b // 8) % 2. Family f belongs to owner f // 100. Among the 8 blocks of one owner index and one rep index, at most 2 name families of any one owner, and at least one owner has exactly 2 of them.
All inputs are finite; a program needn't handle non-finite values.
Results may differ from a plain program's by a relative error of at most 0.0046.
Values may be sent and summed in bfloat16 or wider, within the bound.
A program may use at most 256 MiB of HBM per device.

v0:
```python
import functools

import jax
import jax.numpy as jnp
from jax import lax
from jax.experimental import pallas as pl
from jax.experimental.pallas import tpu as pltpu
from jax.sharding import PartitionSpec as P


BLK = 128
CAP = 2


adapter_scale = 2.0
F32 = jnp.float32
BF16 = jnp.bfloat16


def slot_order(homes):
    count = homes.shape[-1]
    same = homes[..., :, None] == homes[..., None, :]
    iota = jnp.arange(count, dtype=jnp.int32)
    lower = iota[None, :] < iota[:, None]
    return jnp.sum((same & lower).astype(jnp.int32), axis=-1)


def swap(x, axis, size, step):
    return lax.ppermute(x, axis, [(i, i ^ step) for i in range(size)])


def dot_nt(a, b):
    return lax.dot_general(a, b, (((1,), (1,)), ((), ())), preferred_element_type=F32)


def dot_tn(a, b):
    return lax.dot_general(a, b, (((0,), (0,)), ((), ())), preferred_element_type=F32)


def gather_kernel(ids, table_ref, out_ref):
    out_ref[...] = table_ref[...]


def gather_panels(ids, table, n_owner):
    rank, cols = table.shape[1:]
    spec = pl.BlockSpec((1, rank, cols), lambda i, ids: (ids[i], 0, 0))
    out = pl.pallas_call(
        gather_kernel,
        grid_spec=pltpu.PrefetchScalarGridSpec(
            num_scalar_prefetch=1,
            grid=(n_owner * CAP,),
            in_specs=[spec],
            out_specs=pl.BlockSpec((1, rank, cols), lambda i, ids: (i, 0, 0)),
        ),
        out_shape=jax.ShapeDtypeStruct((n_owner * CAP, rank, cols), BF16),
    )(ids, table)
    return out.reshape(n_owner, CAP, rank, cols)


def panel_spec(rank, cols, step=1, at=0):
    return pl.BlockSpec(
        (1, 1, rank, cols),
        lambda j, place: (place[0, j * step + at], place[1, j * step + at], 0, 0),
    )


def low_kernel(scale, place, x_ref, pan_ref, out_ref):
    out_ref[...] = scale * dot_nt(x_ref[...], pan_ref[0, 0])


def low_parts(scale, place, x, panels):
    rank, cols = panels.shape[2:]
    rows = x.shape[0]
    return pl.pallas_call(
        functools.partial(low_kernel, scale),
        grid_spec=pltpu.PrefetchScalarGridSpec(
            num_scalar_prefetch=1,
            grid=(rows // BLK,),
            in_specs=[
                pl.BlockSpec((BLK, cols), lambda j, place: (j, 0)),
                panel_spec(rank, cols),
            ],
            out_specs=pl.BlockSpec((BLK, rank), lambda j, place: (j, 0)),
        ),
        out_shape=jax.ShapeDtypeStruct((rows, rank), F32),
    )(place, x, panels)


def term_kernel(scale, place, low_ref, x_ref, out_ref):
    n_rep, _, half = out_ref.shape[1:4]
    rep = place[2, 0]
    terms = (scale * dot_tn(low_ref[...], x_ref[...])).astype(BF16)
    for h in range(n_rep):
        out_ref[0, rep ^ h, 0] = terms[h * half : (h + 1) * half]


def grad_terms(scale, place, low, x, n_owner, n_rep):
    rows, cols = x.shape
    rank = low.shape[1]
    half = rank // n_rep
    return pl.pallas_call(
        functools.partial(term_kernel, scale),
        grid_spec=pltpu.PrefetchScalarGridSpec(
            num_scalar_prefetch=1,
            grid=(rows // BLK,),
            in_specs=[
                pl.BlockSpec((BLK, rank), lambda j, place: (j, 0)),
                pl.BlockSpec((BLK, cols), lambda j, place: (j, 0)),
            ],
            out_specs=pl.BlockSpec(
                (1, n_rep, 1, half, cols),
                lambda j, place: (place[0, j], 0, place[1, j], 0, 0),
            ),
        ),
        out_shape=jax.ShapeDtypeStruct((n_owner, n_rep, CAP, half, cols), BF16),
    )(place, low, x)


def scatter_kernel(fams, *refs):
    out_ref = refs[-1]
    step = out_ref.shape[0]
    base = pl.program_id(0) * step
    out_ref[...] = jnp.zeros_like(out_ref)
    for k, recv_ref in enumerate(refs[:-1]):
        for c in range(CAP):
            spot = fams[k * CAP + c] - base

            @pl.when((spot >= 0) & (spot < step))
            def _(recv_ref=recv_ref, c=c, spot=spot):
                out_ref[spot] += recv_ref[c].astype(F32)


def scatter_families(fams, recvs, fam_own):
    half, cols = recvs[0].shape[1:]
    step = next(s for s in (20, 10, 5, 4, 2, 1) if fam_own % s == 0)
    return pl.pallas_call(
        scatter_kernel,
        grid_spec=pltpu.PrefetchScalarGridSpec(
            num_scalar_prefetch=1,
            grid=(fam_own // step,),
            in_specs=[pl.BlockSpec(recvs[0].shape, lambda i, fams: (0, 0, 0))] * len(recvs),
            out_specs=pl.BlockSpec((step, half, cols), lambda i, fams: (i, 0, 0)),
        ),
        out_shape=jax.ShapeDtypeStruct((fam_own, half, cols), F32),
    )(fams, *recvs)


def own_kernel(dot, scale, group, count, place, low_ref, *refs):
    pans, xs, ws = refs[:group], refs[group : group + count], refs[group + count : -1]
    out_ref = refs[-1]
    total = dot(xs[0][...], ws[0][...])
    for x, w in zip(xs[1:], ws[1:]):
        total += dot(x[...], w[...])
    for g in range(group):
        at = slice(g * BLK, (g + 1) * BLK)
        extra = jnp.dot(low_ref[at], pans[g][0, 0], preferred_element_type=F32)
        out_ref[at] = total[at] + scale * extra


def own_sums(dot, scale, place, low, panels, xs, ws):
    rank, cols = panels.shape[2:]
    rows = xs[0].shape[0]
    group = 2 if rows % (2 * BLK) == 0 else 1
    height = group * BLK
    row_spec = pl.BlockSpec((height, cols), lambda j, place: (j, 0))
    return pl.pallas_call(
        functools.partial(own_kernel, dot, scale, group, len(xs)),
        grid_spec=pltpu.PrefetchScalarGridSpec(
            num_scalar_prefetch=1,
            grid=(rows // height,),
            in_specs=[pl.BlockSpec((height, rank), lambda j, place: (j, 0))]
            + [panel_spec(rank, cols, group, g) for g in range(group)]
            + [row_spec] * len(xs)
            + [pl.BlockSpec(ws[0].shape, lambda j, place: (0, 0))] * len(ws),
            out_specs=row_spec,
        ),
        out_shape=jax.ShapeDtypeStruct((rows, cols), F32),
    )(place, low, *[panels] * group, *xs, *ws)


def dot_nn(a, b):
    return jnp.dot(a, b, preferred_element_type=F32)


def tables(family_ids, owner, rep, n_owner, n_rep, fam_own):
    fam = family_ids.reshape(n_owner, n_rep, -1)
    homes = fam // fam_own
    slots = slot_order(homes)
    cap_iota = jnp.arange(CAP, dtype=jnp.int32)
    hit = (homes == owner)[..., None] & (slots[..., None] == cap_iota)
    local = fam - owner * fam_own
    sent = jnp.sum(jnp.where(hit, local[..., None] + 1, 0), axis=2) - 1
    o_iota = jnp.arange(n_owner, dtype=jnp.int32)
    r_iota = jnp.arange(n_rep, dtype=jnp.int32)
    o_sel = (o_iota[:, None] ^ owner) == o_iota[None, :]
    r_sel = (r_iota[:, None] ^ rep) == r_iota[None, :]
    pick = o_sel[:, None, :, None] & r_sel[None, :, None, :]
    rel = jnp.sum(jnp.where(pick[..., None], sent[None, None], 0), axis=(2, 3))
    mine = (o_iota == owner)[:, None, None] & (r_iota == rep)[None, :, None]
    my_home = jnp.sum(jnp.where(mine, homes, 0), axis=(0, 1))
    my_slot = jnp.sum(jnp.where(mine, slots, 0), axis=(0, 1))
    place = jnp.stack([my_home ^ owner, my_slot, jnp.full_like(my_slot, rep)])
    return rel.astype(jnp.int32), place.astype(jnp.int32)


def shards(tokens, frozen_weight, adapter_down, adapter_up, cotangent, family_ids):
    n_owner, n_tok, n_rep = (lax.axis_size(a) for a in ("owner", "tok", "rep"))
    owner, tok, rep = (lax.axis_index(a) for a in ("owner", "tok", "rep"))
    rows, cols = tokens.shape
    fam_own = adapter_down.shape[0]
    inner = 1 << ((n_tok.bit_length() - 1) // 2)
    outer = n_tok // inner
    b = tok % inner

    cot_rel = [cotangent] + [
        swap(cotangent, "tok", n_tok, ar * inner) for ar in range(1, outer)
    ]

    quarter = cols // (2 * n_rep)
    parity = owner % 2
    row_at = (rep * 2 + parity) * quarter
    weight_rel = []
    first = []
    for br in range(inner):
        col_at = [(((tok // inner) ^ ar) * inner + (b ^ br)) * cols for ar in range(outer)]
        if br == 0:
            weight_rel.append(
                [lax.dynamic_slice(frozen_weight, (0, at), (cols, cols)) for at in col_at]
            )
            continue
        piece = jnp.concatenate(
            [lax.dynamic_slice(frozen_weight, (row_at, at), (quarter, cols)) for at in col_at]
        )
        first.append(swap(piece, "tok", n_tok, br))

    rel, place = tables(family_ids, owner, rep, n_owner, n_rep, fam_own)
    ids = jnp.maximum(rel[:, 0], 0).reshape(-1)

    def fetch(send):
        return [send[0]] + [
            swap(send[s], "owner", n_owner, s) for s in range(1, n_owner)
        ]

    send_down = gather_panels(ids, adapter_down, n_owner)
    send_up = gather_panels(ids, adapter_up, n_owner)
    got_down = fetch(send_down)
    got_down, send_up = lax.optimization_barrier((got_down, send_up))
    got_up = fetch(send_up)
    down_panels = jnp.stack(got_down)
    up_panels = jnp.stack(got_up)

    tokens_after = tokens
    if first:
        tokens_after, first = lax.optimization_barrier((tokens, first))
    tok_rel = [tokens] + [
        swap(tokens_after, "tok", n_tok, br) for br in range(1, inner)
    ]
    for piece in first:
        other = swap(piece, "owner", n_owner, 1)
        lo = jnp.where(parity == 0, piece, other)
        hi = jnp.where(parity == 0, other, piece)
        mine = jnp.stack([lo, hi])
        theirs = swap(mine, "rep", n_rep, 1)
        both = [jnp.where(rep == r, mine, theirs) for r in range(n_rep)]
        weight_rel.append(
            [
                jnp.concatenate(
                    [
                        both[r][e, ar * quarter : (ar + 1) * quarter]
                        for r in range(n_rep)
                        for e in range(2)
                    ]
                )
                for ar in range(outer)
            ]
        )

    piece_rows = rows // n_tok

    def rows_of(x, t):
        return lax.dynamic_slice_in_dim(x, t * piece_rows, piece_rows, 0)

    def sum_tok(part):
        total = rows_of(part, tok)
        for s in range(1, n_tok):
            total = total + swap(rows_of(part, tok ^ s), "tok", n_tok, s)
        total = total.astype(BF16)
        low = jnp.zeros(part.shape, BF16)
        for s in range(n_tok):
            got = swap(total, "tok", n_tok, s) if s else total
            low = lax.dynamic_update_slice_in_dim(low, got, (tok ^ s) * piece_rows, 0)
        return low

    def to_owners(terms):
        recvs = []
        for s in range(n_owner):
            for rs in range(n_rep):
                term = terms[s, rs]
                if s or rs:
                    pairs = [
                        (o * n_rep + r, (o ^ s) * n_rep + (r ^ rs))
                        for o in range(n_owner)
                        for r in range(n_rep)
                    ]
                    term = lax.ppermute(term, ("owner", "rep"), pairs)
                recvs.append(term)
        return recvs

    fams = rel.reshape(-1)
    low = sum_tok(low_parts(1.0, place, tokens, down_panels))
    up_terms = grad_terms(adapter_scale, place, low, cotangent, n_owner, n_rep)
    up_recv = to_owners(up_terms)
    grad_low = sum_tok(low_parts(adapter_scale, place, cotangent, up_panels))
    down_terms = grad_terms(1.0, place, grad_low, tokens, n_owner, n_rep)
    down_recv = to_owners(down_terms)

    def partial(dot, xs, ws):
        acc = None
        for x, w in zip(xs, ws):
            d = dot(x, w)
            acc = d if acc is None else acc + d
        return acc.astype(BF16)

    back_recv = [
        swap(partial(dot_nt, cot_rel, weight_rel[br]), "tok", n_tok, br)
        for br in range(1, inner)
    ]
    base_recv = [
        swap(
            partial(dot_nn, tok_rel, [w[ar] for w in weight_rel]),
            "tok", n_tok, ar * inner,
        )
        for ar in range(1, outer)
    ]
    back = own_sums(dot_nt, 1.0, place, grad_low, down_panels, cot_rel, weight_rel[0])
    base = own_sums(
        dot_nn, adapter_scale, place, low, up_panels, tok_rel,
        [w[0] for w in weight_rel],
    )
    grad_up = scatter_families(fams, up_recv, fam_own)
    grad_down = scatter_families(fams, down_recv, fam_own)

    def finish(own, recvs):
        for r in recvs:
            own = own + r.astype(F32)
        return own.astype(BF16)

    return (finish(base, base_recv), finish(back, back_recv), grad_down, grad_up)


def solution(mesh):
    in_specs = (
        P(("owner", "rep"), "tok"),
        P("tok", None),
        P("owner", None, "tok"),
        P("owner", None, "tok"),
        P(("owner", "rep"), "tok"),
        P(),
    )
    out_specs = (
        P(("owner", "rep"), "tok"),
        P(("owner", "rep"), "tok"),
        P("owner", "rep", "tok"),
        P("owner", "rep", "tok"),
    )

    return jax.shard_map(
        shards, mesh=mesh, in_specs=in_specs, out_specs=out_specs, check_vma=False
    )
```

profile of v0, /device:TPU:0, one launch (start us, length us, event | category | flops | bytes accessed | tf_op | source)
XLA Modules:
  0.0 334.1 jit_solution(4297076761225420408)
XLA Ops:
  2.1 3.0 collective-permute-start.12
  6.2 22.0 %collective-permute-done.12 = bf16[512,1024]{1,0:T(8,128)(2,1)S(1)} collective-permute-done((bf16[512,1024]{1,0:T(8,128)(2,1)S(1)}, bf16[512,1024]{1,0:T(8,128)(2,1)S(1)}, u32[]{:S(2)}, u32[]{:S(2)}) %collective-permute-start.12) | collective-permute-done | bytes 1048608 | tf_op jit(solution)/shard_map/ppermute | solution.py:29
  28.2 1.8 collective-permute-start.14
  31.1 5.9 %shard_map.93 = bf16[8,64,1024]{2,1,0:T(8,128)(2,1)} custom-call(s32[8]{0:T(128)} %max.8.ids, bf16[100,64,1024]{2,1,0:T(8,128)(2,1)} %table_ref.2), custom_call_target="tpu_custom_call" | custom-call | tf_op jit(solution)/shard_map/pallas_call | solution.py:47
  36.9 2.2 fusion.9
  39.2 2.5 collective-permute-start.2
  41.8 1.8 collective-permute-start
  45.2 5.9 %shard_map.94 = bf16[8,64,1024]{2,1,0:T(8,128)(2,1)} custom-call(s32[8]{0:T(128)} %max.8.ids, bf16[100,64,1024]{2,1,0:T(8,128)(2,1)} %table_ref.3), custom_call_target="tpu_custom_call" | custom-call | tf_op jit(solution)/shard_map/pallas_call | solution.py:47
  51.6 14.0 %collective-permute-done.14 = bf16[512,1024]{1,0:T(8,128)(2,1)} collective-permute-done((bf16[512,1024]{1,0:T(8,128)(2,1)S(1)}, bf16[512,1024]{1,0:T(8,128)(2,1)}, u32[]{:S(2)}, u32[]{:S(2)}) %collective-permute-start.14) | collective-permute-done | bytes 1048608 | tf_op jit(solution)/shard_map/ppermute | solution.py:29
  69.0 4.7 %constant_dynamic-slice_fusion.3 = (bf16[1024,1024]{1,0:T(8,128)(2,1)}, bf16[1024,1024]{1,0:T(8,128)(2,1)}) fusion(bf16[1024,4096]{1,0:T(8,128)(2,1)} %param.7, s32[]{:T(128)S(6)} %select_n.138, s32[]{:T(128)S(6)} %select_n.130), kind=kLoop, calls=%fused_computation.59 | loop fusion | bytes 8388616 | tf_op jit(solution)/shard_map/dynamic_slice | solution.py:228
  73.7 2.3 pad_maximum_fusion.3.pan_ref.refs_0_.refs_1_
  75.9 6.9 %shard_map.95 = f32[1024,64]{1,0:T(8,128)} custom-call(s32[3,8]{1,0:T(4,128)} %add_add_fusion.place, bf16[1024,1024]{1,0:T(8,128)(2,1)} %x_ref.6, bf16[4,2,64,1024]{3,2,1,0:T(8,128)(2,1)} %pad_maximum_fusion.3.pan_ref.refs_0_.refs_1_), custom_call_target="tpu_custom_call" | custom-call | tf_op jit(solution)/shard_map/pallas_call | solution.py:74
  88.1 6.6 %fusion.10 = f32[1024,1024]{0,1:T(8,128)} fusion(bf16[1024,1024]{1,0:T(8,128)(2,1)} %x_ref.6, bf16[1024,1024]{1,0:T(8,128)(2,1)} %get-tuple-element.26.refs_5_), kind=kOutput, calls=%fused_computation.93 | convolution fusion | flops 2147483648 | bytes 8388608 | tf_op jit(solution)/shard_map/dot_general | solution.py:182
  100.7 2.2 fusion.8
  102.9 3.6 %collective-permute-start.11 = (bf16[2,64,1024]{2,1,0:T(8,128)(2,1)}, bf16[2,64,1024]{2,1,0:T(8,128)(2,1)}, u32[]{:S(2)}, u32[]{:S(2)}) collective-permute-start(bf16[2,64,1024]{2,1,0:T(8,128)(2,1)} %get-tuple-element.59), channel_id=1, source_target_pairs={{0,24},{8,16},{16,8},{24,0},{1,25},{9,17},{17,9},{25,1},{2,26},{10... | collective-permute-start | bytes 786440 | tf_op jit(solution)/shard_map/ppermute | solution.py:29
  108.1 6.9 %shard_map.101 = bf16[4,2,2,32,1024]{4,3,2,1,0:T(8,128)(2,1)} custom-call(s32[3,8]{1,0:T(4,128)} %add_add_fusion.place, bf16[1024,64]{1,0:T(8,128)(2,1)} %copy-done.6, bf16[1024,1024]{1,0:T(8,128)(2,1)} %x_ref.7), custom_call_target="tpu_custom_call" | custom-call | tf_op jit(solution)/shard_map/pallas_call | solution.py:101
  115.1 11.4 %collective-permute-done.10 = bf16[2,64,1024]{2,1,0:T(8,128)(2,1)} collective-permute-done((bf16[2,64,1024]{2,1,0:T(8,128)(2,1)}, bf16[2,64,1024]{2,1,0:T(8,128)(2,1)}, u32[]{:S(2)}, u32[]{:S(2)}) %collective-permute-start.10) | collective-permute-done | bytes 262176 | tf_op jit(solution)/shard_map/ppermute | solution.py:29
  126.4 2.3 pad_maximum_fusion.4.refs_0_.refs_1_.pan_ref
  128.7 6.9 %shard_map.97 = f32[1024,64]{1,0:T(8,128)} custom-call(s32[3,8]{1,0:T(4,128)} %add_add_fusion.place, bf16[1024,1024]{1,0:T(8,128)(2,1)} %x_ref.7, bf16[4,2,64,1024]{3,2,1,0:T(8,128)(2,1)} %pad_maximum_fusion.4.refs_0_.refs_1_.pan_ref), custom_call_target="tpu_custom_call" | custom-call | tf_op jit(solution)/shard_map/pallas_call | solution.py:74
  138.8 2.4 collective-permute-start.19
  141.8 2.1 broadcast_select_fusion.1
  144.5 4.4 %fusion.2 = f32[1024,1024]{0,1:T(8,128)S(1)} fusion(bf16[1024,1024]{1,0:T(8,128)(2,1)} %collective-permute-done.23.refs_3_, bf16[256,1024]{1,0:T(8,128)(2,1)S(1)} %get-tuple-element.37, bf16[256,1024]{1,0:T(8,128)(2,1)S(1)} %get-tuple-element.36, bf16[256,1024]{1,0:T(8,128)(2,1)S(1)} %get-tuple-element.77, bf16[256,1024]{1,0:T(8,128)(2,1)S(1)} %get-tuple-element.78), kind=kOutput, calls=%fused_computation.24 | convolution fusion | flops 2155872256 | bytes 8388608 | tf_op jit(solution)/shard_map/dot_general | solution.py:33
  148.9 3.7 %fusion.1 = bf16[1024,1024]{1,0:T(8,128)(2,1)} fusion(f32[1024,1024]{0,1:T(8,128)S(1)} %fusion.2, bf16[1024,1024]{1,0:T(8,128)(2,1)S(1)} %copy-done.1, bf16[256,1024]{1,0:T(8,128)(2,1)S(1)} %get-tuple-element.38, bf16[256,1024]{1,0:T(8,128)(2,1)S(1)} %get-tuple-element.39, bf16[256,1024]{1,0:T(8,128)(2,1)S(1)} %get-tuple-element.76, ...), kind=kOutput, calls=%fused_computation.5 | convolution fusion | flops 2157969408 | bytes 10485760 | tf_op jit(solution)/shard_map/dot_general | solution.py:33
  153.2 31.2 %collective-permute-done.13.refs_3_ = bf16[1024,1024]{1,0:T(8,128)(2,1)S(1)} collective-permute-done((bf16[1024,1024]{1,0:T(8,128)(2,1)}, bf16[1024,1024]{1,0:T(8,128)(2,1)S(1)}, u32[]{:S(2)}, u32[]{:S(2)}) %collective-permute-start.13) | collective-permute-done | bytes 2097184 | tf_op jit(solution)/shard_map/ppermute | solution.py:29
  184.4 3.6 %fusion = bf16[1024,1024]{1,0:T(8,128)(2,1)} fusion(f32[1024,1024]{0,1:T(8,128)S(1)} %copy-done.18, bf16[1024,1024]{1,0:T(8,128)(2,1)S(1)} %collective-permute-done.13.refs_3_, bf16[256,1024]{1,0:T(8,128)(2,1)S(1)} %get-tuple-element.37, bf16[256,1024]{1,0:T(8,128)(2,1)S(1)} %get-tuple-element.36, bf16[256,1024]{1,0:T(8,128)(2,1)S(1)} %get-tuple-element.77, ...), kind=kOutput, calls=%fused_computation.1 | convolution fusion | flops 2157969408 | bytes 10485760 | tf_op jit(solution)/shard_map/dot_general | solution.py:182
  194.4 2.7 collective-permute-start.37
  197.1 36.2 %collective-permute-done.20 = bf16[256,64]{1,0:T(8,128)(2,1)S(1)} collective-permute-done((bf16[256,64]{1,0:T(8,128)(2,1)S(1)}, bf16[256,64]{1,0:T(8,128)(2,1)S(1)}, u32[]{:S(2)}, u32[]{:S(2)}) %collective-permute-start.20) | collective-permute-done | bytes 32800 | tf_op jit(solution)/shard_map/ppermute | solution.py:29
  233.3 1.8 collective-permute-start.21
  235.1 2.5 collective-permute-done.21
  237.6 3.4 %collective-permute-start.22 = (bf16[256,64]{1,0:T(8,128)(2,1)S(1)}, bf16[256,64]{1,0:T(8,128)(2,1)S(1)}, u32[]{:S(2)}, u32[]{:S(2)}) collective-permute-start(bf16[256,64]{1,0:T(8,128)(2,1)S(1)} %get-tuple-element.21), channel_id=1, source_target_pairs={{0,6},{2,4},{4,2},{6,0},{1,7},{3,5},{5,3},{7,1},{8,14},{10,12},{12... | collective-permute-start | bytes 98312 | tf_op jit(solution)/shard_map/ppermute | solution.py:29
  241.0 2.2 collective-permute-done.22
  244.0 6.9 %shard_map.99 = bf16[4,2,2,32,1024]{4,3,2,1,0:T(8,128)(2,1)} custom-call(s32[3,8]{1,0:T(4,128)} %add_add_fusion.place, bf16[1024,64]{1,0:T(8,128)(2,1)} %copy-done.5, bf16[1024,1024]{1,0:T(8,128)(2,1)} %x_ref.6), custom_call_target="tpu_custom_call" | custom-call | tf_op jit(solution)/shard_map/pallas_call | solution.py:101
  251.1 2.7 collective-permute-start.34
  253.8 2.1 slice_bitcast_fusion.19
  257.6 3.2 collective-permute-done.35.refs_4_
  260.8 2.3 collective-permute-start.31
  263.7 2.2 collective-permute-start.30
  265.9 2.1 collective-permute-done.31.refs_7_
  268.1 7.9 %collective-permute-start.28 = (bf16[2,32,1024]{2,1,0:T(8,128)(2,1)S(1)}, bf16[2,32,1024]{2,1,0:T(8,128)(2,1)}, u32[]{:S(2)}, u32[]{:S(2)}) collective-permute-start(bf16[2,32,1024]{2,1,0:T(8,128)(2,1)S(1)} %get-tuple-element.53), channel_id=1, source_target_pairs={{0,16},{1,17},{8,24},{9,25},{16,0},{17,1},{24,8},{25,9},{2,18},{3,... | collective-permute-start | bytes 393224 | tf_op jit(solution)/shard_map/ppermute | solution.py:305
  277.7 5.7 %collective-permute-done.29.refs_5_ = bf16[2,32,1024]{2,1,0:T(8,128)(2,1)} collective-permute-done((bf16[2,32,1024]{2,1,0:T(8,128)(2,1)S(1)}, bf16[2,32,1024]{2,1,0:T(8,128)(2,1)}, u32[]{:S(2)}, u32[]{:S(2)}) %collective-permute-start.29) | collective-permute-done | bytes 131104 | tf_op jit(solution)/shard_map/ppermute | solution.py:305
  283.4 2.5 collective-permute-done.28.refs_4_
  286.8 7.5 %shard_map.102 = f32[100,32,1024]{2,1,0:T(8,128)} custom-call(s32[16]{0:T(128)} %reshape.208.fams, bf16[2,32,1024]{2,1,0:T(8,128)(2,1)} %get-tuple-element.49.refs_0_, bf16[2,32,1024]{2,1,0:T(8,128)(2,1)} %collective-permute-done.32.refs_1_, bf16[2,32,1024]{2,1,0:T(8,128)(2,1)} %collective-permute-done.33.refs_2_, bf16[2,32,1024]{2,1,0:T(8,128)(2,1)} %copy-done.13, ...), custom_call_target="tpu_custom_call" | custom-call | tf_op jit(solution)/shard_map/pallas_call | solution.py:136
  294.2 7.5 %shard_map.100 = f32[100,32,1024]{2,1,0:T(8,128)} custom-call(s32[16]{0:T(128)} %reshape.208.fams, bf16[2,32,1024]{2,1,0:T(8,128)(2,1)} %get-tuple-element.57.refs_0_, bf16[2,32,1024]{2,1,0:T(8,128)(2,1)} %collective-permute-done.25.refs_1_, bf16[2,32,1024]{2,1,0:T(8,128)(2,1)} %collective-permute-done.26.refs_2_, ...), custom_call_target="tpu_custom_call" | custom-call | tf_op jit(solution)/shard_map/pallas_call | solution.py:136
  301.7 10.6 %shard_map.98 = f32[1024,1024]{1,0:T(8,128)} custom-call(s32[3,8]{1,0:T(4,128)} %add_add_fusion.place, bf16[1024,64]{1,0:T(8,128)(2,1)} %copy-done.5, bf16[4,2,64,1024]{3,2,1,0:T(8,128)(2,1)} %pad_maximum_fusion.3.pan_ref.refs_0_.refs_1_, bf16[4,2,64,1024]{3,2,1,0:T(8,128)(2,1)} %pad_maximum_fusion.3.pan_ref.refs_0_.refs_1_, bf16[1024,1024]{1,0:T(8,128)(2,1)} %x_ref.7, ...), custom_call_target="tpu_custom_call" | custom-call | tf_op jit(solution)/shard_map/pallas_call | solution.py:166
  312.3 2.7 pad_maximum_fusion.1.refs_5_
  315.0 10.9 %shard_map.96 = f32[1024,1024]{1,0:T(8,128)} custom-call(s32[3,8]{1,0:T(4,128)} %add_add_fusion.place, bf16[1024,64]{1,0:T(8,128)(2,1)} %copy-done.6, bf16[4,2,64,1024]{3,2,1,0:T(8,128)(2,1)} %pad_maximum_fusion.4.refs_0_.refs_1_.pan_ref, bf16[4,2,64,1024]{3,2,1,0:T(8,128)(2,1)} %pad_maximum_fusion.4.refs_0_.refs_1_.pan_ref, bf16[1024,1024]{1,0:T(8,128)(2,1)} %x_ref.6, ...), custom_call_target="tpu_custom_call" | custom-call | tf_op jit(solution)/shard_map/pallas_call | solution.py:166
  325.9 4.4 %add_convert_fusion = bf16[1024,1024]{1,0:T(8,128)(2,1)} fusion(f32[1024,1024]{1,0:T(8,128)} %shard_map.98, bf16[1024,1024]{1,0:T(8,128)(2,1)S(1)} %collective-permute-done.24), kind=kLoop, calls=%fused_computation.2 | loop fusion | flops 3145728 | bytes 8388608 | tf_op jit(solution)/shard_map/convert_element_type | solution.py:346
  330.3 3.8 %add_convert_fusion.2 = bf16[1024,1024]{1,0:T(8,128)(2,1)} fusion(f32[1024,1024]{1,0:T(8,128)S(1)} %copy-done.2, bf16[1024,1024]{1,0:T(8,128)(2,1)} %collective-permute-done.16), kind=kLoop, calls=%fused_computation.4 | loop fusion | flops 3145728 | bytes 8388608 | tf_op jit(solution)/shard_map/convert_element_type | solution.py:346
  (140 shorter events, 39.0 us)
Async XLA Ops:
  2.1 26.2 %collective-permute-start.12 = (bf16[512,1024]{1,0:T(8,128)(2,1)S(1)}, bf16[512,1024]{1,0:T(8,128)(2,1)S(1)}, u32[]{:S(2)}, u32[]{:S(2)}) collective-permute-start(bf16[512,1024]{1,0:T(8,128)(2,1)S(1)} %pad_maximum_fusion.5), channel_id=1, source_target_pairs={{0,2},{2,0},{4,6},{6,4},{1,3},{3,1},{5,7},{7,5},{8,10},{10,8},{12,... | collective-permute-start | bytes 3145736 | tf_op jit(solution)/shard_map/ppermute | solution.py:29
  28.2 8.7 %copy-start.10 = (bf16[512,1024]{1,0:T(8,128)(2,1)}, bf16[512,1024]{1,0:T(8,128)(2,1)S(1)}, u32[]{:S(2)}) copy-start(bf16[512,1024]{1,0:T(8,128)(2,1)S(1)} %collective-permute-done.12) | copy-start | bytes 3145732
  28.2 37.4 %collective-permute-start.14 = (bf16[512,1024]{1,0:T(8,128)(2,1)S(1)}, bf16[512,1024]{1,0:T(8,128)(2,1)}, u32[]{:S(2)}, u32[]{:S(2)}) collective-permute-start(bf16[512,1024]{1,0:T(8,128)(2,1)S(1)} %collective-permute-done.12), channel_id=1, source_target_pairs={{0,8},{8,0},{16,24},{24,16},{1,9},{9,1},{17,25},{25,17},{2,10},{10... | collective-permute-start | bytes 3145736 | tf_op jit(solution)/shard_map/ppermute | solution.py:29
  36.9 6.6 %copy-start = (bf16[1024,1024]{1,0:T(8,128)(2,1)S(1)}, bf16[1024,1024]{1,0:T(8,128)(2,1)}, u32[]{:S(2)}) copy-start(bf16[1024,1024]{1,0:T(8,128)(2,1)} %x_ref.7) | copy-start | bytes 6291460
  39.2 34.5 %collective-permute-start.2 = (bf16[2,64,1024]{2,1,0:T(8,128)(2,1)}, bf16[2,64,1024]{2,1,0:T(8,128)(2,1)}, u32[]{:S(2)}, u32[]{:S(2)}) collective-permute-start(bf16[2,64,1024]{2,1,0:T(8,128)(2,1)} %get-tuple-element.62), channel_id=1, source_target_pairs={{0,24},{8,16},{16,8},{24,0},{1,25},{9,17},{17,9},{25,1},{2,26},{10... | collective-permute-start | bytes 786440 | tf_op jit(solution)/shard_map/ppermute | solution.py:29
  41.6 32.0 %collective-permute-start.1 = (bf16[2,64,1024]{2,1,0:T(8,128)(2,1)}, bf16[2,64,1024]{2,1,0:T(8,128)(2,1)}, u32[]{:S(2)}, u32[]{:S(2)}) collective-permute-start(bf16[2,64,1024]{2,1,0:T(8,128)(2,1)} %get-tuple-element.63), channel_id=1, source_target_pairs={{0,16},{8,24},{16,0},{24,8},{1,17},{9,25},{17,1},{25,9},{2,18},{10... | collective-permute-start | bytes 786440 | tf_op jit(solution)/shard_map/ppermute | solution.py:29
  41.8 31.9 %collective-permute-start = (bf16[2,64,1024]{2,1,0:T(8,128)(2,1)}, bf16[2,64,1024]{2,1,0:T(8,128)(2,1)}, u32[]{:S(2)}, u32[]{:S(2)}) collective-permute-start(bf16[2,64,1024]{2,1,0:T(8,128)(2,1)} %get-tuple-element.64), channel_id=1, source_target_pairs={{0,8},{8,0},{16,24},{24,16},{1,9},{9,1},{17,25},{25,17},{2,10},{10... | collective-permute-start | bytes 786440 | tf_op jit(solution)/shard_map/ppermute | solution.py:29
  43.6 100.9 %collective-permute-start.23 = (bf16[1024,1024]{1,0:T(8,128)(2,1)S(1)}, bf16[1024,1024]{1,0:T(8,128)(2,1)}, u32[]{:S(2)}, u32[]{:S(2)}) collective-permute-start(bf16[1024,1024]{1,0:T(8,128)(2,1)S(1)} %copy-done), channel_id=1, source_target_pairs={{0,4},{2,6},{4,0},{6,2},{1,5},{3,7},{5,1},{7,3},{8,12},{10,14},{12... | collective-permute-start | bytes 6291464 | tf_op jit(solution)/shard_map/ppermute | solution.py:29
  69.0 72.3 %collective-permute-start.15 = (bf16[2,512,1024]{2,1,0:T(8,128)(2,1)}, bf16[2,512,1024]{2,1,0:T(8,128)(2,1)}, u32[]{:S(2)}, u32[]{:S(2)}) collective-permute-start(bf16[2,512,1024]{2,1,0:T(8,128)(2,1)} %pad_maximum_fusion), channel_id=1, source_target_pairs={{0,1},{1,0},{2,3},{3,2},{4,5},{5,4},{6,7},{7,6},{8,9},{9,8},{10,11... | collective-permute-start | bytes 6291464 | tf_op jit(solution)/shard_map/ppermute | solution.py:29
  84.6 10.1 %collective-permute-start.3 = (f32[256,64]{1,0:T(8,128)}, f32[256,64]{1,0:T(8,128)S(1)}, u32[]{:S(2)}, u32[]{:S(2)}) collective-permute-start(f32[256,64]{1,0:T(8,128)} %get-tuple-element.69), channel_id=1, source_target_pairs={{0,2},{2,0},{4,6},{6,4},{1,3},{3,1},{5,7},{7,5},{8,10},{10,8},{12,... | collective-permute-start | bytes 196616 | tf_op jit(solution)/shard_map/ppermute | solution.py:29
  86.3 8.5 %collective-permute-start.5 = (f32[256,64]{1,0:T(8,128)}, f32[256,64]{1,0:T(8,128)S(1)}, u32[]{:S(2)}, u32[]{:S(2)}) collective-permute-start(f32[256,64]{1,0:T(8,128)} %get-tuple-element.70), channel_id=1, source_target_pairs={{0,6},{2,4},{4,2},{6,0},{1,7},{3,5},{5,3},{7,1},{8,14},{10,12},{12... | collective-permute-start | bytes 196616 | tf_op jit(solution)/shard_map/ppermute | solution.py:29
  87.8 8.3 %collective-permute-start.4 = (f32[256,64]{1,0:T(8,128)S(1)}, f32[256,64]{1,0:T(8,128)}, u32[]{:S(2)}, u32[]{:S(2)}) collective-permute-start(f32[256,64]{1,0:T(8,128)S(1)} %get-tuple-element.71), channel_id=1, source_target_pairs={{0,4},{2,6},{4,0},{6,2},{1,5},{3,7},{5,1},{7,3},{8,12},{10,14},{12... | collective-permute-start | bytes 196616 | tf_op jit(solution)/shard_map/ppermute | solution.py:29
  97.2 5.8 %collective-permute-start.7 = (bf16[256,64]{1,0:T(8,128)(2,1)S(1)}, bf16[256,64]{1,0:T(8,128)(2,1)S(1)}, u32[]{:S(2)}, u32[]{:S(2)}) collective-permute-start(bf16[256,64]{1,0:T(8,128)(2,1)S(1)} %get-tuple-element.23), channel_id=1, source_target_pairs={{0,4},{2,6},{4,0},{6,2},{1,5},{3,7},{5,1},{7,3},{8,12},{10,14},{12... | collective-permute-start | bytes 98312 | tf_op jit(solution)/shard_map/ppermute | solution.py:29
  98.2 8.3 %collective-permute-start.6 = (bf16[256,64]{1,0:T(8,128)(2,1)S(1)}, bf16[256,64]{1,0:T(8,128)(2,1)S(1)}, u32[]{:S(2)}, u32[]{:S(2)}) collective-permute-start(bf16[256,64]{1,0:T(8,128)(2,1)S(1)} %get-tuple-element.23), channel_id=1, source_target_pairs={{0,2},{2,0},{4,6},{6,4},{1,3},{3,1},{5,7},{7,5},{8,10},{10,8},{12,... | collective-permute-start | bytes 98312 | tf_op jit(solution)/shard_map/ppermute | solution.py:29
  99.7 6.8 %collective-permute-start.8 = (bf16[256,64]{1,0:T(8,128)(2,1)S(1)}, bf16[256,64]{1,0:T(8,128)(2,1)S(1)}, u32[]{:S(2)}, u32[]{:S(2)}) collective-permute-start(bf16[256,64]{1,0:T(8,128)(2,1)S(1)} %get-tuple-element.23), channel_id=1, source_target_pairs={{0,6},{2,4},{4,2},{6,0},{1,7},{3,5},{5,3},{7,1},{8,14},{10,12},{12... | collective-permute-start | bytes 98312 | tf_op jit(solution)/shard_map/ppermute | solution.py:29
  102.9 12.1 %collective-permute-start.11 = (bf16[2,64,1024]{2,1,0:T(8,128)(2,1)}, bf16[2,64,1024]{2,1,0:T(8,128)(2,1)}, u32[]{:S(2)}, u32[]{:S(2)}) collective-permute-start(bf16[2,64,1024]{2,1,0:T(8,128)(2,1)} %get-tuple-element.59), channel_id=1, source_target_pairs={{0,24},{8,16},{16,8},{24,0},{1,25},{9,17},{17,9},{25,1},{2,26},{10... | collective-permute-start | bytes 786440 | tf_op jit(solution)/shard_map/ppermute | solution.py:29
  106.5 19.9 %collective-permute-start.10 = (bf16[2,64,1024]{2,1,0:T(8,128)(2,1)}, bf16[2,64,1024]{2,1,0:T(8,128)(2,1)}, u32[]{:S(2)}, u32[]{:S(2)}) collective-permute-start(bf16[2,64,1024]{2,1,0:T(8,128)(2,1)} %get-tuple-element.60), channel_id=1, source_target_pairs={{0,16},{8,24},{16,0},{24,8},{1,17},{9,25},{17,1},{25,9},{2,18},{10... | collective-permute-start | bytes 786440 | tf_op jit(solution)/shard_map/ppermute | solution.py:29
  106.5 19.9 %collective-permute-start.9 = (bf16[2,64,1024]{2,1,0:T(8,128)(2,1)}, bf16[2,64,1024]{2,1,0:T(8,128)(2,1)}, u32[]{:S(2)}, u32[]{:S(2)}) collective-permute-start(bf16[2,64,1024]{2,1,0:T(8,128)(2,1)} %get-tuple-element.61), channel_id=1, source_target_pairs={{0,8},{8,0},{16,24},{24,16},{1,9},{9,1},{17,25},{25,17},{2,10},{10... | collective-permute-start | bytes 786440 | tf_op jit(solution)/shard_map/ppermute | solution.py:29
  135.6 48.7 %collective-permute-start.13 = (bf16[1024,1024]{1,0:T(8,128)(2,1)}, bf16[1024,1024]{1,0:T(8,128)(2,1)S(1)}, u32[]{:S(2)}, u32[]{:S(2)}) collective-permute-start(bf16[1024,1024]{1,0:T(8,128)(2,1)} %x_ref.6), channel_id=1, source_target_pairs={{0,2},{2,0},{4,6},{6,4},{1,3},{3,1},{5,7},{7,5},{8,10},{10,8},{12,... | collective-permute-start | bytes 6291464 | tf_op jit(solution)/shard_map/ppermute | solution.py:29
  138.2 51.4 %collective-permute-start.17 = (f32[256,64]{1,0:T(8,128)S(1)}, f32[256,64]{1,0:T(8,128)S(1)}, u32[]{:S(2)}, u32[]{:S(2)}) collective-permute-start(f32[256,64]{1,0:T(8,128)S(1)} %get-tuple-element.66), channel_id=1, source_target_pairs={{0,2},{2,0},{4,6},{6,4},{1,3},{3,1},{5,7},{7,5},{8,10},{10,8},{12,... | collective-permute-start | bytes 196616 | tf_op jit(solution)/shard_map/ppermute | solution.py:29
  138.8 52.2 %collective-permute-start.19 = (f32[256,64]{1,0:T(8,128)S(1)}, f32[256,64]{1,0:T(8,128)S(1)}, u32[]{:S(2)}, u32[]{:S(2)}) collective-permute-start(f32[256,64]{1,0:T(8,128)S(1)} %get-tuple-element.67), channel_id=1, source_target_pairs={{0,6},{2,4},{4,2},{6,0},{1,7},{3,5},{5,3},{7,1},{8,14},{10,12},{12... | collective-permute-start | bytes 196616 | tf_op jit(solution)/shard_map/ppermute | solution.py:29
  141.2 49.7 %collective-permute-start.18 = (f32[256,64]{1,0:T(8,128)S(1)}, f32[256,64]{1,0:T(8,128)S(1)}, u32[]{:S(2)}, u32[]{:S(2)}) collective-permute-start(f32[256,64]{1,0:T(8,128)S(1)} %get-tuple-element.68), channel_id=1, source_target_pairs={{0,4},{2,6},{4,0},{6,2},{1,5},{3,7},{5,1},{7,3},{8,12},{10,14},{12... | collective-permute-start | bytes 196616 | tf_op jit(solution)/shard_map/ppermute | solution.py:29
  148.9 35.4 %copy-start.18 = (f32[1024,1024]{0,1:T(8,128)S(1)}, f32[1024,1024]{0,1:T(8,128)}, u32[]{:S(2)}) copy-start(f32[1024,1024]{0,1:T(8,128)} %fusion.10) | copy-start | bytes 12582916
  152.6 40.9 %copy-start.4 = (bf16[4,2,2,32,1024]{4,3,2,1,0:T(8,128)(2,1)S(1)}, bf16[4,2,2,32,1024]{4,3,2,1,0:T(8,128)(2,1)}, u32[]{:S(2)}) copy-start(bf16[4,2,2,32,1024]{4,3,2,1,0:T(8,128)(2,1)} %shard_map.101) | copy-start | bytes 3145732
  152.6 173.2 %collective-permute-start.24 = (bf16[1024,1024]{1,0:T(8,128)(2,1)}, bf16[1024,1024]{1,0:T(8,128)(2,1)S(1)}, u32[]{:S(2)}, u32[]{:S(2)}) collective-permute-start(bf16[1024,1024]{1,0:T(8,128)(2,1)} %fusion.1), channel_id=1, source_target_pairs={{0,2},{2,0},{4,6},{6,4},{1,3},{3,1},{5,7},{7,5},{8,10},{10,8},{12,... | collective-permute-start | bytes 6291464 | tf_op jit(solution)/shard_map/ppermute | solution.py:29
  188.0 142.3 %collective-permute-start.16 = (bf16[1024,1024]{1,0:T(8,128)(2,1)}, bf16[1024,1024]{1,0:T(8,128)(2,1)}, u32[]{:S(2)}, u32[]{:S(2)}) collective-permute-start(bf16[1024,1024]{1,0:T(8,128)(2,1)} %fusion), channel_id=1, source_target_pairs={{0,4},{2,6},{4,0},{6,2},{1,5},{3,7},{5,1},{7,3},{8,12},{10,14},{12... | collective-permute-start | bytes 6291464 | tf_op jit(solution)/shard_map/ppermute | solution.py:29
  191.9 41.4 %collective-permute-start.20 = (bf16[256,64]{1,0:T(8,128)(2,1)S(1)}, bf16[256,64]{1,0:T(8,128)(2,1)S(1)}, u32[]{:S(2)}, u32[]{:S(2)}) collective-permute-start(bf16[256,64]{1,0:T(8,128)(2,1)S(1)} %get-tuple-element.21), channel_id=1, source_target_pairs={{0,2},{2,0},{4,6},{6,4},{1,3},{3,1},{5,7},{7,5},{8,10},{10,8},{12,... | collective-permute-start | bytes 98312 | tf_op jit(solution)/shard_map/ppermute | solution.py:29
  194.4 56.5 %collective-permute-start.38 = (bf16[2,32,1024]{2,1,0:T(8,128)(2,1)}, bf16[2,32,1024]{2,1,0:T(8,128)(2,1)S(1)}, u32[]{:S(2)}, u32[]{:S(2)}) collective-permute-start(bf16[2,32,1024]{2,1,0:T(8,128)(2,1)} %get-tuple-element.42), channel_id=1, source_target_pairs={{0,25},{1,24},{8,17},{9,16},{16,9},{17,8},{24,1},{25,0},{2,27},{3,... | collective-permute-start | bytes 393224 | tf_op jit(solution)/shard_map/ppermute | solution.py:305
  194.4 56.6 %collective-permute-start.37 = (bf16[2,32,1024]{2,1,0:T(8,128)(2,1)}, bf16[2,32,1024]{2,1,0:T(8,128)(2,1)}, u32[]{:S(2)}, u32[]{:S(2)}) collective-permute-start(bf16[2,32,1024]{2,1,0:T(8,128)(2,1)} %get-tuple-element.43), channel_id=1, source_target_pairs={{0,24},{1,25},{8,16},{9,17},{16,8},{17,9},{24,0},{25,1},{2,26},{3,... | collective-permute-start | bytes 393224 | tf_op jit(solution)/shard_map/ppermute | solution.py:305
  233.3 4.3 %collective-permute-start.21 = (bf16[256,64]{1,0:T(8,128)(2,1)S(1)}, bf16[256,64]{1,0:T(8,128)(2,1)S(1)}, u32[]{:S(2)}, u32[]{:S(2)}) collective-permute-start(bf16[256,64]{1,0:T(8,128)(2,1)S(1)} %get-tuple-element.21), channel_id=1, source_target_pairs={{0,4},{2,6},{4,0},{6,2},{1,5},{3,7},{5,1},{7,3},{8,12},{10,14},{12... | collective-permute-start | bytes 98312 | tf_op jit(solution)/shard_map/ppermute | solution.py:29
  237.6 5.7 %collective-permute-start.22 = (bf16[256,64]{1,0:T(8,128)(2,1)S(1)}, bf16[256,64]{1,0:T(8,128)(2,1)S(1)}, u32[]{:S(2)}, u32[]{:S(2)}) collective-permute-start(bf16[256,64]{1,0:T(8,128)(2,1)S(1)} %get-tuple-element.21), channel_id=1, source_target_pairs={{0,6},{2,4},{4,2},{6,0},{1,7},{3,5},{5,3},{7,1},{8,14},{10,12},{12... | collective-permute-start | bytes 98312 | tf_op jit(solution)/shard_map/ppermute | solution.py:29
  243.3 12.6 %collective-permute-start.36 = (bf16[2,32,1024]{2,1,0:T(8,128)(2,1)}, bf16[2,32,1024]{2,1,0:T(8,128)(2,1)}, u32[]{:S(2)}, u32[]{:S(2)}) collective-permute-start(bf16[2,32,1024]{2,1,0:T(8,128)(2,1)} %get-tuple-element.44), channel_id=1, source_target_pairs={{0,17},{1,16},{8,25},{9,24},{16,1},{17,0},{24,9},{25,8},{2,19},{3,... | collective-permute-start | bytes 393224 | tf_op jit(solution)/shard_map/ppermute | solution.py:305
  251.0 4.9 %copy-start.15 = (bf16[2,32,1024]{2,1,0:T(8,128)(2,1)S(1)}, bf16[2,32,1024]{2,1,0:T(8,128)(2,1)}, u32[]{:S(2)}) copy-start(bf16[2,32,1024]{2,1,0:T(8,128)(2,1)} %get-tuple-element.47) | copy-start | bytes 393220
  251.0 9.8 %copy-start.14 = (bf16[2,32,1024]{2,1,0:T(8,128)(2,1)S(1)}, bf16[2,32,1024]{2,1,0:T(8,128)(2,1)}, u32[]{:S(2)}) copy-start(bf16[2,32,1024]{2,1,0:T(8,128)(2,1)} %get-tuple-element.48) | copy-start | bytes 393220
  251.0 35.8 %copy-start.11 = (bf16[2,32,1024]{2,1,0:T(8,128)(2,1)}, bf16[2,32,1024]{2,1,0:T(8,128)(2,1)S(1)}, u32[]{:S(2)}) copy-start(bf16[2,32,1024]{2,1,0:T(8,128)(2,1)S(1)} %collective-permute-done.38.refs_7_) | copy-start | bytes 393220
  251.0 9.8 %collective-permute-start.35 = (bf16[2,32,1024]{2,1,0:T(8,128)(2,1)}, bf16[2,32,1024]{2,1,0:T(8,128)(2,1)S(1)}, u32[]{:S(2)}, u32[]{:S(2)}) collective-permute-start(bf16[2,32,1024]{2,1,0:T(8,128)(2,1)} %get-tuple-element.45), channel_id=1, source_target_pairs={{0,16},{1,17},{8,24},{9,25},{16,0},{17,1},{24,8},{25,9},{2,18},{3,... | collective-permute-start | bytes 393224 | tf_op jit(solution)/shard_map/ppermute | solution.py:305
  251.1 9.7 %collective-permute-start.34 = (bf16[2,32,1024]{2,1,0:T(8,128)(2,1)}, bf16[2,32,1024]{2,1,0:T(8,128)(2,1)S(1)}, u32[]{:S(2)}, u32[]{:S(2)}) collective-permute-start(bf16[2,32,1024]{2,1,0:T(8,128)(2,1)} %get-tuple-element.46), channel_id=1, source_target_pairs={{0,9},{1,8},{8,1},{9,0},{16,25},{17,24},{24,17},{25,16},{2,11},{3,... | collective-permute-start | bytes 393224 | tf_op jit(solution)/shard_map/ppermute | solution.py:305
  255.9 7.8 %collective-permute-start.33 = (bf16[2,32,1024]{2,1,0:T(8,128)(2,1)S(1)}, bf16[2,32,1024]{2,1,0:T(8,128)(2,1)}, u32[]{:S(2)}, u32[]{:S(2)}) collective-permute-start(bf16[2,32,1024]{2,1,0:T(8,128)(2,1)S(1)} %copy-done.15), channel_id=1, source_target_pairs={{0,8},{1,9},{8,0},{9,1},{16,24},{17,25},{24,16},{25,17},{2,10},{3,... | collective-permute-start | bytes 393224 | tf_op jit(solution)/shard_map/ppermute | solution.py:305
  260.8 26.0 %copy-start.12 = (bf16[2,32,1024]{2,1,0:T(8,128)(2,1)}, bf16[2,32,1024]{2,1,0:T(8,128)(2,1)S(1)}, u32[]{:S(2)}) copy-start(bf16[2,32,1024]{2,1,0:T(8,128)(2,1)S(1)} %collective-permute-done.35.refs_4_) | copy-start | bytes 393220
  260.8 5.1 %collective-permute-start.32 = (bf16[2,32,1024]{2,1,0:T(8,128)(2,1)S(1)}, bf16[2,32,1024]{2,1,0:T(8,128)(2,1)}, u32[]{:S(2)}, u32[]{:S(2)}) collective-permute-start(bf16[2,32,1024]{2,1,0:T(8,128)(2,1)S(1)} %copy-done.14), channel_id=1, source_target_pairs={{0,1},{1,0},{8,9},{9,8},{16,17},{17,16},{24,25},{25,24},{2,3},{3,2... | collective-permute-start | bytes 393224 | tf_op jit(solution)/shard_map/ppermute | solution.py:305
  260.8 26.0 %copy-start.13 = (bf16[2,32,1024]{2,1,0:T(8,128)(2,1)}, bf16[2,32,1024]{2,1,0:T(8,128)(2,1)S(1)}, u32[]{:S(2)}) copy-start(bf16[2,32,1024]{2,1,0:T(8,128)(2,1)S(1)} %collective-permute-done.34.refs_3_) | copy-start | bytes 393220
  260.8 7.3 %collective-permute-start.31 = (bf16[2,32,1024]{2,1,0:T(8,128)(2,1)S(1)}, bf16[2,32,1024]{2,1,0:T(8,128)(2,1)}, u32[]{:S(2)}, u32[]{:S(2)}) collective-permute-start(bf16[2,32,1024]{2,1,0:T(8,128)(2,1)S(1)} %get-tuple-element.50), channel_id=1, source_target_pairs={{0,25},{1,24},{8,17},{9,16},{16,9},{17,8},{24,1},{25,0},{2,27},{3,... | collective-permute-start | bytes 393224 | tf_op jit(solution)/shard_map/ppermute | solution.py:305
  263.7 12.2 %collective-permute-start.30 = (bf16[2,32,1024]{2,1,0:T(8,128)(2,1)S(1)}, bf16[2,32,1024]{2,1,0:T(8,128)(2,1)}, u32[]{:S(2)}, u32[]{:S(2)}) collective-permute-start(bf16[2,32,1024]{2,1,0:T(8,128)(2,1)S(1)} %get-tuple-element.51), channel_id=1, source_target_pairs={{0,24},{1,25},{8,16},{9,17},{16,8},{17,9},{24,0},{25,1},{2,26},{3,... | collective-permute-start | bytes 393224 | tf_op jit(solution)/shard_map/ppermute | solution.py:305
  265.9 17.5 %collective-permute-start.29 = (bf16[2,32,1024]{2,1,0:T(8,128)(2,1)S(1)}, bf16[2,32,1024]{2,1,0:T(8,128)(2,1)}, u32[]{:S(2)}, u32[]{:S(2)}) collective-permute-start(bf16[2,32,1024]{2,1,0:T(8,128)(2,1)S(1)} %get-tuple-element.52), channel_id=1, source_target_pairs={{0,17},{1,16},{8,25},{9,24},{16,1},{17,0},{24,9},{25,8},{2,19},{3,... | collective-permute-start | bytes 393224 | tf_op jit(solution)/shard_map/ppermute | solution.py:305
  268.1 17.9 %collective-permute-start.28 = (bf16[2,32,1024]{2,1,0:T(8,128)(2,1)S(1)}, bf16[2,32,1024]{2,1,0:T(8,128)(2,1)}, u32[]{:S(2)}, u32[]{:S(2)}) collective-permute-start(bf16[2,32,1024]{2,1,0:T(8,128)(2,1)S(1)} %get-tuple-element.53), channel_id=1, source_target_pairs={{0,16},{1,17},{8,24},{9,25},{16,0},{17,1},{24,8},{25,9},{2,18},{3,... | collective-permute-start | bytes 393224 | tf_op jit(solution)/shard_map/ppermute | solution.py:305
  276.0 18.3 %collective-permute-start.27 = (bf16[2,32,1024]{2,1,0:T(8,128)(2,1)}, bf16[2,32,1024]{2,1,0:T(8,128)(2,1)}, u32[]{:S(2)}, u32[]{:S(2)}) collective-permute-start(bf16[2,32,1024]{2,1,0:T(8,128)(2,1)} %get-tuple-element.54), channel_id=1, source_target_pairs={{0,9},{1,8},{8,1},{9,0},{16,25},{17,24},{24,17},{25,16},{2,11},{3,... | collective-permute-start | bytes 393224 | tf_op jit(solution)/shard_map/ppermute | solution.py:305
  283.4 10.8 %collective-permute-start.26 = (bf16[2,32,1024]{2,1,0:T(8,128)(2,1)}, bf16[2,32,1024]{2,1,0:T(8,128)(2,1)}, u32[]{:S(2)}, u32[]{:S(2)}) collective-permute-start(bf16[2,32,1024]{2,1,0:T(8,128)(2,1)} %get-tuple-element.55), channel_id=1, source_target_pairs={{0,8},{1,9},{8,0},{9,1},{16,24},{17,25},{24,16},{25,17},{2,10},{3,... | collective-permute-start | bytes 393224 | tf_op jit(solution)/shard_map/ppermute | solution.py:305
  286.0 8.3 %collective-permute-start.25 = (bf16[2,32,1024]{2,1,0:T(8,128)(2,1)}, bf16[2,32,1024]{2,1,0:T(8,128)(2,1)}, u32[]{:S(2)}, u32[]{:S(2)}) collective-permute-start(bf16[2,32,1024]{2,1,0:T(8,128)(2,1)} %get-tuple-element.56), channel_id=1, source_target_pairs={{0,1},{1,0},{8,9},{9,8},{16,17},{17,16},{24,25},{25,24},{2,3},{3,2... | collective-permute-start | bytes 393224 | tf_op jit(solution)/shard_map/ppermute | solution.py:305
  (10 other events, 29.6 us)
where the time goes:
time: 336 us; the launch traced here: 334 us
  waiting for transfers between devices  136 us (40%)
  Pallas kernels  75.8 us (23%)
  starting transfers between devices  57.5 us (17%)
  other arithmetic  24.7 us (7%)
  local copies, waits for them, and re-layouts  21 us (6%)
  matrix products  18.3 us (5%)
    ppermute x25, waiting for transfers between devices, swap(): return lax.ppermute(x, axis, [(i, i ^ step) for i in range(size)])  122 us
    ppermute x25, starting transfers between devices, swap(): return lax.ppermute(x, axis, [(i, i ^ step) for i in range(size)])  36.1 us
    pallas_call x2, Pallas kernels, own_sums(): pl.pallas_call(functools.partial(own_kernel, dot, scale, group, len(xs)),...  21.5 us
    ppermute x14, starting transfers between devices, to_owners(): term = lax.ppermute(term, ('owner', 'rep'), pairs)  21.4 us
    pallas_call x2, Pallas kernels, scatter_families(): pl.pallas_call(scatter_kernel, grid_spec=pltpu.PrefetchScalarGridSpec(num...  14.9 us
    ppermute x14, waiting for transfers between devices, to_owners(): term = lax.ppermute(term, ('owner', 'rep'), pairs)  14.1 us
    pallas_call x2, Pallas kernels, grad_terms(): pl.pallas_call(functools.partial(term_kernel, scale), grid_spec=pltpu.Pre...  13.9 us
    pallas_call x2, Pallas kernels, low_parts(): pl.pallas_call(functools.partial(low_kernel, scale), grid_spec=pltpu.Pref...  13.8 us
  transfers between devices with their start and end apart: 39, of which 15 were waited for; matrix products, arithmetic and copies ran while one was open for 17% of the time, Pallas kernels for 23%

commit v1 on v0

--- a/solution.py
+++ b/solution.py
@@ -37,23 +37,27 @@
     return lax.dot_general(a, b, (((0,), (0,)), ((), ())), preferred_element_type=F32)
 
 
-def gather_kernel(ids, table_ref, out_ref):
-    out_ref[...] = table_ref[...]
+def gather_kernel(count, ids, *refs):
+    for k in range(count):
+        refs[count][k] = refs[k][0]
 
 
 def gather_panels(ids, table, n_owner):
     rank, cols = table.shape[1:]
-    spec = pl.BlockSpec((1, rank, cols), lambda i, ids: (ids[i], 0, 0))
+    count = n_owner * CAP
+    specs = [
+        pl.BlockSpec((1, rank, cols), lambda i, ids, k=k: (ids[k], 0, 0)) for k in range(count)
+    ]
     out = pl.pallas_call(
-        gather_kernel,
-        grid_spec=pltpu.PrefetchScalarGridSpec(
-            num_scalar_prefetch=1,
-            grid=(n_owner * CAP,),
-            in_specs=[spec],
-            out_specs=pl.BlockSpec((1, rank, cols), lambda i, ids: (i, 0, 0)),
-        ),
-        out_shape=jax.ShapeDtypeStruct((n_owner * CAP, rank, cols), BF16),
-    )(ids, table)
+        functools.partial(gather_kernel, count),
+        grid_spec=pltpu.PrefetchScalarGridSpec(
+            num_scalar_prefetch=1,
+            grid=(1,),
+            in_specs=specs,
+            out_specs=pl.BlockSpec((count, rank, cols), lambda i, ids: (0, 0, 0)),
+        ),
+        out_shape=jax.ShapeDtypeStruct((count, rank, cols), BF16),
+    )(ids, *[table] * count)
     return out.reshape(n_owner, CAP, rank, cols)
 
 
@@ -64,55 +68,54 @@
     )
 
 
+def whole_spec(shape):
+    return pl.BlockSpec(shape, lambda i, place: (0,) * len(shape))
+
+
 def low_kernel(scale, place, x_ref, pan_ref, out_ref):
-    out_ref[...] = scale * dot_nt(x_ref[...], pan_ref[0, 0])
+    for j in range(x_ref.shape[0] // BLK):
+        at = slice(j * BLK, (j + 1) * BLK)
+        panel = pan_ref[place[0, j], place[1, j]]
+        out_ref[at] = scale * dot_nt(x_ref[at], panel)
 
 
 def low_parts(scale, place, x, panels):
-    rank, cols = panels.shape[2:]
-    rows = x.shape[0]
+    out_shape = (x.shape[0], panels.shape[2])
     return pl.pallas_call(
         functools.partial(low_kernel, scale),
         grid_spec=pltpu.PrefetchScalarGridSpec(
             num_scalar_prefetch=1,
-            grid=(rows // BLK,),
-            in_specs=[
-                pl.BlockSpec((BLK, cols), lambda j, place: (j, 0)),
-                panel_spec(rank, cols),
-            ],
-            out_specs=pl.BlockSpec((BLK, rank), lambda j, place: (j, 0)),
-        ),
-        out_shape=jax.ShapeDtypeStruct((rows, rank), F32),
+            grid=(1,),
+            in_specs=[whole_spec(x.shape), whole_spec(panels.shape)],
+            out_specs=whole_spec(out_shape),
+        ),
+        out_shape=jax.ShapeDtypeStruct(out_shape, F32),
     )(place, x, panels)
 
 
 def term_kernel(scale, place, low_ref, x_ref, out_ref):
     n_rep, _, half = out_ref.shape[1:4]
     rep = place[2, 0]
-    terms = (scale * dot_tn(low_ref[...], x_ref[...])).astype(BF16)
-    for h in range(n_rep):
-        out_ref[0, rep ^ h, 0] = terms[h * half : (h + 1) * half]
+    for j in range(x_ref.shape[0] // BLK):
+        at = slice(j * BLK, (j + 1) * BLK)
+        terms = (scale * dot_tn(low_ref[at], x_ref[at])).astype(BF16)
+        for h in range(n_rep):
+            out_ref[place[0, j], rep ^ h, place[1, j]] = terms[h * half : (h + 1) * half]
 
 
 def grad_terms(scale, place, low, x, n_owner, n_rep):
-    rows, cols = x.shape
-    rank = low.shape[1]
-    half = rank // n_rep
+    cols = x.shape[1]
+    half = low.shape[1] // n_rep
+    out_shape = (n_owner, n_rep, CAP, half, cols)
     return pl.pallas_call(
         functools.partial(term_kernel, scale),
         grid_spec=pltpu.PrefetchScalarGridSpec(
             num_scalar_prefetch=1,
-            grid=(rows // BLK,),
-            in_specs=[
-                pl.BlockSpec((BLK, rank), lambda j, place: (j, 0)),
-                pl.BlockSpec((BLK, cols), lambda j, place: (j, 0)),
-            ],
-            out_specs=pl.BlockSpec(
-                (1, n_rep, 1, half, cols),
-                lambda j, place: (place[0, j], 0, place[1, j], 0, 0),
-            ),
-        ),
-        out_shape=jax.ShapeDtypeStruct((n_owner, n_rep, CAP, half, cols), BF16),
+            grid=(1,),
+            in_specs=[whole_spec(low.shape), whole_spec(x.shape)],
+            out_specs=whole_spec(out_shape),
+        ),
+        out_shape=jax.ShapeDtypeStruct(out_shape, BF16),
     )(place, low, x)
 
 
@@ -212,9 +215,7 @@
     outer = n_tok // inner
     b = tok % inner
 
-    cot_rel = [cotangent] + [
-        swap(cotangent, "tok", n_tok, ar * inner) for ar in range(1, outer)
-    ]
+    cot_rel = [cotangent] + [swap(cotangent, "tok", n_tok, ar * inner) for ar in range(1, outer)]
 
     quarter = cols // (2 * n_rep)
     parity = owner % 2
@@ -237,9 +238,7 @@
     ids = jnp.maximum(rel[:, 0], 0).reshape(-1)
 
     def fetch(send):
-        return [send[0]] + [
-            swap(send[s], "owner", n_owner, s) for s in range(1, n_owner)
-        ]
+        return [send[0]] + [swap(send[s], "owner", n_owner, s) for s in range(1, n_owner)]
 
     send_down = gather_panels(ids, adapter_down, n_owner)
     send_up = gather_panels(ids, adapter_up, n_owner)
@@ -252,9 +251,7 @@
     tokens_after = tokens
     if first:
         tokens_after, first = lax.optimization_barrier((tokens, first))
-    tok_rel = [tokens] + [
-        swap(tokens_after, "tok", n_tok, br) for br in range(1, inner)
-    ]
+    tok_rel = [tokens] + [swap(tokens_after, "tok", n_tok, br) for br in range(1, inner)]
     for piece in first:
         other = swap(piece, "owner", n_owner, 1)
         lo = jnp.where(parity == 0, piece, other)
@@ -364,6 +361,4 @@
         P("owner", "rep", "tok"),
     )
 
-    return jax.shard_map(
-        shards, mesh=mesh, in_specs=in_specs, out_specs=out_specs, check_vma=False
-    )
+    return jax.shard_map(shards, mesh=mesh, in_specs=in_specs, out_specs=out_specs, check_vma=False)

time: 336 us -> 326 us (0.970)
  Pallas kernels: 75.8 us -> 57.8 us
  waiting for transfers between devices: 136 us -> 145 us
    ppermute x25, waiting for transfers between devices: 122 us -> 131 us  [swap(): return lax.ppermute(x, axis, [(i, i ^ step) for i in range(size)])]
    pallas_call x2, Pallas kernels: 13.9 us -> 7.63 us  [grad_terms(): pl.pallas_call(functools.partial(term_kernel, scale), grid_spec=pltpu.Pre...]
    pallas_call x2, Pallas kernels: 11.7 us -> 5.97 us  [gather_panels(): pl.pallas_call(functools.partial(gather_kernel, count), grid_spec=pltpu.P...]
    pallas_call x2, Pallas kernels: 13.8 us -> 8.07 us  [low_parts(): pl.pallas_call(functools.partial(low_kernel, scale), grid_spec=pltpu.Pref...]
  transfers between devices with their start and end apart: 39 -> 39, of which waited for: 15 -> 16; matrix products, arithmetic and copies ran while one was open for 17% -> 17% of each run, Pallas kernels for 23% -> 18%
where the time goes in v1:
time: 326 us; the launch traced here: 325 us
  waiting for transfers between devices  145 us (44%)
  Pallas kernels  57.8 us (18%)
  starting transfers between devices  57.4 us (18%)
  other arithmetic  24.7 us (8%)
  local copies, waits for them, and re-layouts  21 us (6%)
  matrix products  18.3 us (6%)
    ppermute x25, waiting for transfers between devices, swap(): return lax.ppermute(x, axis, [(i, i ^ step) for i in range(size)])  131 us
    ppermute x25, starting transfers between devices, swap(): return lax.ppermute(x, axis, [(i, i ^ step) for i in range(size)])  36 us
    ppermute x14, starting transfers between devices, to_owners(): term = lax.ppermute(term, ('owner', 'rep'), pairs)  21.4 us
    pallas_call x2, Pallas kernels, own_sums(): pl.pallas_call(functools.partial(own_kernel, dot, scale, group, len(xs)),...  21.3 us
    pallas_call x2, Pallas kernels, scatter_families(): pl.pallas_call(scatter_kernel, grid_spec=pltpu.PrefetchScalarGridSpec(num...  14.9 us
    ppermute x14, waiting for transfers between devices, to_owners(): term = lax.ppermute(term, ('owner', 'rep'), pairs)  14.1 us
    dot_general x2, matrix products, dot_nn(): return jnp.dot(a, b, preferred_element_type=F32)  10.2 us
    convert_element_type x2, other arithmetic, finish(): return own.astype(BF16)  8.22 us
  transfers between devices with their start and end apart: 39, of which 16 were waited for; matrix products, arithmetic and copies ran while one was open for 17% of the time, Pallas kernels for 18%

profile of v1, /device:TPU:0, one launch (start us, length us, event | category | flops | bytes accessed | tf_op | source)
XLA Modules:
  0.0 325.0 jit_solution(10330985147266363020)
XLA Ops:
  2.1 3.0 collective-permute-start.12
  6.2 22.0 %collective-permute-done.12 = bf16[512,1024]{1,0:T(8,128)(2,1)S(1)} collective-permute-done((bf16[512,1024]{1,0:T(8,128)(2,1)S(1)}, bf16[512,1024]{1,0:T(8,128)(2,1)S(1)}, u32[]{:S(2)}, u32[]{:S(2)}) %collective-permute-start.12) | collective-permute-done | bytes 1048608 | tf_op jit(solution)/shard_map/ppermute | solution.py:29
  28.2 1.8 collective-permute-start.14
  31.1 3.0 shard_map.93
  34.1 2.2 fusion.9
  36.3 2.5 collective-permute-start.2
  38.9 1.8 collective-permute-start
  42.3 3.0 shard_map.94
  45.9 19.7 %collective-permute-done.14 = bf16[512,1024]{1,0:T(8,128)(2,1)} collective-permute-done((bf16[512,1024]{1,0:T(8,128)(2,1)S(1)}, bf16[512,1024]{1,0:T(8,128)(2,1)}, u32[]{:S(2)}, u32[]{:S(2)}) %collective-permute-start.14) | collective-permute-done | bytes 1048608 | tf_op jit(solution)/shard_map/ppermute | solution.py:29
  69.0 4.7 %constant_dynamic-slice_fusion.3 = (bf16[1024,1024]{1,0:T(8,128)(2,1)}, bf16[1024,1024]{1,0:T(8,128)(2,1)}) fusion(bf16[1024,4096]{1,0:T(8,128)(2,1)} %param.7, s32[]{:T(128)S(6)} %select_n.138, s32[]{:T(128)S(6)} %select_n.130), kind=kLoop, calls=%fused_computation.59 | loop fusion | bytes 8388616 | tf_op jit(solution)/shard_map/dynamic_slice | solution.py:229
  73.7 2.3 pad_maximum_fusion.3.pan_ref.refs_0_.refs_1_
  75.9 4.0 %shard_map.95 = f32[1024,64]{1,0:T(8,128)} custom-call(s32[3,8]{1,0:T(4,128)} %add_add_fusion.place, bf16[1024,1024]{1,0:T(8,128)(2,1)} %x_ref.6, bf16[4,2,64,1024]{3,2,1,0:T(8,128)(2,1)} %pad_maximum_fusion.3.pan_ref.refs_0_.refs_1_), custom_call_target="tpu_custom_call" | custom-call | tf_op jit(solution)/shard_map/pallas_call | solution.py:84
  85.2 6.6 %fusion.10 = f32[1024,1024]{0,1:T(8,128)} fusion(bf16[1024,1024]{1,0:T(8,128)(2,1)} %x_ref.6, bf16[1024,1024]{1,0:T(8,128)(2,1)} %get-tuple-element.26.refs_5_), kind=kOutput, calls=%fused_computation.93 | convolution fusion | flops 2147483648 | bytes 8388608 | tf_op jit(solution)/shard_map/dot_general | solution.py:185
  97.9 2.2 fusion.8
  100.1 3.6 %collective-permute-start.11 = (bf16[2,64,1024]{2,1,0:T(8,128)(2,1)}, bf16[2,64,1024]{2,1,0:T(8,128)(2,1)}, u32[]{:S(2)}, u32[]{:S(2)}) collective-permute-start(bf16[2,64,1024]{2,1,0:T(8,128)(2,1)} %get-tuple-element.59), channel_id=1, source_target_pairs={{0,24},{8,16},{16,8},{24,0},{1,25},{9,17},{17,9},{25,1},{2,26},{10... | collective-permute-start | bytes 786440 | tf_op jit(solution)/shard_map/ppermute | solution.py:29
  105.3 3.8 %shard_map.101 = bf16[4,2,2,32,1024]{4,3,2,1,0:T(8,128)(2,1)} custom-call(s32[3,8]{1,0:T(4,128)} %add_add_fusion.place, bf16[1024,64]{1,0:T(8,128)(2,1)} %copy-done.6, bf16[1024,1024]{1,0:T(8,128)(2,1)} %x_ref.7), custom_call_target="tpu_custom_call" | custom-call | tf_op jit(solution)/shard_map/pallas_call | solution.py:110
  109.1 2.4 collective-permute-done.11
  111.5 12.1 %collective-permute-done.10 = bf16[2,64,1024]{2,1,0:T(8,128)(2,1)} collective-permute-done((bf16[2,64,1024]{2,1,0:T(8,128)(2,1)}, bf16[2,64,1024]{2,1,0:T(8,128)(2,1)}, u32[]{:S(2)}, u32[]{:S(2)}) %collective-permute-start.10) | collective-permute-done | bytes 262176 | tf_op jit(solution)/shard_map/ppermute | solution.py:29
  123.6 2.3 pad_maximum_fusion.4.refs_0_.refs_1_.pan_ref
  125.9 4.0 %shard_map.97 = f32[1024,64]{1,0:T(8,128)} custom-call(s32[3,8]{1,0:T(4,128)} %add_add_fusion.place, bf16[1024,1024]{1,0:T(8,128)(2,1)} %x_ref.7, bf16[4,2,64,1024]{3,2,1,0:T(8,128)(2,1)} %pad_maximum_fusion.4.refs_0_.refs_1_.pan_ref), custom_call_target="tpu_custom_call" | custom-call | tf_op jit(solution)/shard_map/pallas_call | solution.py:84
  133.1 2.4 collective-permute-start.19
  136.1 2.1 broadcast_select_fusion.1
  138.8 4.4 %fusion.2 = f32[1024,1024]{0,1:T(8,128)S(1)} fusion(bf16[1024,1024]{1,0:T(8,128)(2,1)} %collective-permute-done.23.refs_3_, bf16[256,1024]{1,0:T(8,128)(2,1)S(1)} %get-tuple-element.37, bf16[256,1024]{1,0:T(8,128)(2,1)S(1)} %get-tuple-element.36, bf16[256,1024]{1,0:T(8,128)(2,1)S(1)} %get-tuple-element.77, bf16[256,1024]{1,0:T(8,128)(2,1)S(1)} %get-tuple-element.78), kind=kOutput, calls=%fused_computation.24 | convolution fusion | flops 2155872256 | bytes 8388608 | tf_op jit(solution)/shard_map/dot_general | solution.py:33
  143.2 3.7 %fusion.1 = bf16[1024,1024]{1,0:T(8,128)(2,1)} fusion(f32[1024,1024]{0,1:T(8,128)S(1)} %fusion.2, bf16[1024,1024]{1,0:T(8,128)(2,1)S(1)} %copy-done.1, bf16[256,1024]{1,0:T(8,128)(2,1)S(1)} %get-tuple-element.38, bf16[256,1024]{1,0:T(8,128)(2,1)S(1)} %get-tuple-element.39, bf16[256,1024]{1,0:T(8,128)(2,1)S(1)} %get-tuple-element.76, ...), kind=kOutput, calls=%fused_computation.5 | convolution fusion | flops 2157969408 | bytes 10485760 | tf_op jit(solution)/shard_map/dot_general | solution.py:33
  147.5 31.2 %collective-permute-done.13.refs_3_ = bf16[1024,1024]{1,0:T(8,128)(2,1)S(1)} collective-permute-done((bf16[1024,1024]{1,0:T(8,128)(2,1)}, bf16[1024,1024]{1,0:T(8,128)(2,1)S(1)}, u32[]{:S(2)}, u32[]{:S(2)}) %collective-permute-start.13) | collective-permute-done | bytes 2097184 | tf_op jit(solution)/shard_map/ppermute | solution.py:29
  178.7 3.6 %fusion = bf16[1024,1024]{1,0:T(8,128)(2,1)} fusion(f32[1024,1024]{0,1:T(8,128)S(1)} %copy-done.18, bf16[1024,1024]{1,0:T(8,128)(2,1)S(1)} %collective-permute-done.13.refs_3_, bf16[256,1024]{1,0:T(8,128)(2,1)S(1)} %get-tuple-element.37, bf16[256,1024]{1,0:T(8,128)(2,1)S(1)} %get-tuple-element.36, bf16[256,1024]{1,0:T(8,128)(2,1)S(1)} %get-tuple-element.77, ...), kind=kOutput, calls=%fused_computation.1 | convolution fusion | flops 2157969408 | bytes 10485760 | tf_op jit(solution)/shard_map/dot_general | solution.py:185
  188.7 2.6 collective-permute-start.37
  191.4 36.3 %collective-permute-done.20 = bf16[256,64]{1,0:T(8,128)(2,1)S(1)} collective-permute-done((bf16[256,64]{1,0:T(8,128)(2,1)S(1)}, bf16[256,64]{1,0:T(8,128)(2,1)S(1)}, u32[]{:S(2)}, u32[]{:S(2)}) %collective-permute-start.20) | collective-permute-done | bytes 32800 | tf_op jit(solution)/shard_map/ppermute | solution.py:29
  229.4 2.5 collective-permute-done.21
  231.9 3.4 %collective-permute-start.22 = (bf16[256,64]{1,0:T(8,128)(2,1)S(1)}, bf16[256,64]{1,0:T(8,128)(2,1)S(1)}, u32[]{:S(2)}, u32[]{:S(2)}) collective-permute-start(bf16[256,64]{1,0:T(8,128)(2,1)S(1)} %get-tuple-element.21), channel_id=1, source_target_pairs={{0,6},{2,4},{4,2},{6,0},{1,7},{3,5},{5,3},{7,1},{8,14},{10,12},{12... | collective-permute-start | bytes 98312 | tf_op jit(solution)/shard_map/ppermute | solution.py:29
  235.3 2.2 collective-permute-done.22
  238.3 3.8 %shard_map.99 = bf16[4,2,2,32,1024]{4,3,2,1,0:T(8,128)(2,1)} custom-call(s32[3,8]{1,0:T(4,128)} %add_add_fusion.place, bf16[1024,64]{1,0:T(8,128)(2,1)} %copy-done.5, bf16[1024,1024]{1,0:T(8,128)(2,1)} %x_ref.6), custom_call_target="tpu_custom_call" | custom-call | tf_op jit(solution)/shard_map/pallas_call | solution.py:110
  242.2 2.7 collective-permute-start.34
  245.0 2.1 slice_bitcast_fusion.19
  248.8 3.2 collective-permute-done.35.refs_4_
  252.0 2.3 collective-permute-start.31
  254.9 2.2 collective-permute-start.30
  257.1 2.1 collective-permute-done.31.refs_7_
  259.2 7.9 %collective-permute-start.28 = (bf16[2,32,1024]{2,1,0:T(8,128)(2,1)S(1)}, bf16[2,32,1024]{2,1,0:T(8,128)(2,1)}, u32[]{:S(2)}, u32[]{:S(2)}) collective-permute-start(bf16[2,32,1024]{2,1,0:T(8,128)(2,1)S(1)} %get-tuple-element.53), channel_id=1, source_target_pairs={{0,16},{1,17},{8,24},{9,25},{16,0},{17,1},{24,8},{25,9},{2,18},{3,... | collective-permute-start | bytes 393224 | tf_op jit(solution)/shard_map/ppermute | solution.py:302
  268.9 5.7 %collective-permute-done.29.refs_5_ = bf16[2,32,1024]{2,1,0:T(8,128)(2,1)} collective-permute-done((bf16[2,32,1024]{2,1,0:T(8,128)(2,1)S(1)}, bf16[2,32,1024]{2,1,0:T(8,128)(2,1)}, u32[]{:S(2)}, u32[]{:S(2)}) %collective-permute-start.29) | collective-permute-done | bytes 131104 | tf_op jit(solution)/shard_map/ppermute | solution.py:302
  274.6 2.5 collective-permute-done.28.refs_4_
  277.9 7.5 %shard_map.102 = f32[100,32,1024]{2,1,0:T(8,128)} custom-call(s32[16]{0:T(128)} %reshape.208.fams, bf16[2,32,1024]{2,1,0:T(8,128)(2,1)} %get-tuple-element.49.refs_0_, bf16[2,32,1024]{2,1,0:T(8,128)(2,1)} %collective-permute-done.32.refs_1_, bf16[2,32,1024]{2,1,0:T(8,128)(2,1)} %collective-permute-done.33.refs_2_, bf16[2,32,1024]{2,1,0:T(8,128)(2,1)} %copy-done.13, ...), custom_call_target="tpu_custom_call" | custom-call | tf_op jit(solution)/shard_map/pallas_call | solution.py:139
  285.4 7.5 %shard_map.100 = f32[100,32,1024]{2,1,0:T(8,128)} custom-call(s32[16]{0:T(128)} %reshape.208.fams, bf16[2,32,1024]{2,1,0:T(8,128)(2,1)} %get-tuple-element.57.refs_0_, bf16[2,32,1024]{2,1,0:T(8,128)(2,1)} %collective-permute-done.25.refs_1_, bf16[2,32,1024]{2,1,0:T(8,128)(2,1)} %collective-permute-done.26.refs_2_, ...), custom_call_target="tpu_custom_call" | custom-call | tf_op jit(solution)/shard_map/pallas_call | solution.py:139
  292.9 10.6 %shard_map.98 = f32[1024,1024]{1,0:T(8,128)} custom-call(s32[3,8]{1,0:T(4,128)} %add_add_fusion.place, bf16[1024,64]{1,0:T(8,128)(2,1)} %copy-done.5, bf16[4,2,64,1024]{3,2,1,0:T(8,128)(2,1)} %pad_maximum_fusion.3.pan_ref.refs_0_.refs_1_, bf16[4,2,64,1024]{3,2,1,0:T(8,128)(2,1)} %pad_maximum_fusion.3.pan_ref.refs_0_.refs_1_, bf16[1024,1024]{1,0:T(8,128)(2,1)} %x_ref.7, ...), custom_call_target="tpu_custom_call" | custom-call | tf_op jit(solution)/shard_map/pallas_call | solution.py:169
  303.5 2.7 pad_maximum_fusion.1.refs_5_
  306.2 10.6 %shard_map.96 = f32[1024,1024]{1,0:T(8,128)} custom-call(s32[3,8]{1,0:T(4,128)} %add_add_fusion.place, bf16[1024,64]{1,0:T(8,128)(2,1)} %copy-done.6, bf16[4,2,64,1024]{3,2,1,0:T(8,128)(2,1)} %pad_maximum_fusion.4.refs_0_.refs_1_.pan_ref, bf16[4,2,64,1024]{3,2,1,0:T(8,128)(2,1)} %pad_maximum_fusion.4.refs_0_.refs_1_.pan_ref, bf16[1024,1024]{1,0:T(8,128)(2,1)} %x_ref.6, ...), custom_call_target="tpu_custom_call" | custom-call | tf_op jit(solution)/shard_map/pallas_call | solution.py:169
  316.8 4.4 %add_convert_fusion = bf16[1024,1024]{1,0:T(8,128)(2,1)} fusion(f32[1024,1024]{1,0:T(8,128)} %shard_map.98, bf16[1024,1024]{1,0:T(8,128)(2,1)S(1)} %collective-permute-done.24), kind=kLoop, calls=%fused_computation.2 | loop fusion | flops 3145728 | bytes 8388608 | tf_op jit(solution)/shard_map/convert_element_type | solution.py:343
  321.3 3.8 %add_convert_fusion.2 = bf16[1024,1024]{1,0:T(8,128)(2,1)} fusion(f32[1024,1024]{1,0:T(8,128)S(1)} %copy-done.2, bf16[1024,1024]{1,0:T(8,128)(2,1)} %collective-permute-done.16), kind=kLoop, calls=%fused_computation.4 | loop fusion | flops 3145728 | bytes 8388608 | tf_op jit(solution)/shard_map/convert_element_type | solution.py:343
  (140 shorter events, 40.8 us)
Async XLA Ops:
  2.1 26.2 %collective-permute-start.12 = (bf16[512,1024]{1,0:T(8,128)(2,1)S(1)}, bf16[512,1024]{1,0:T(8,128)(2,1)S(1)}, u32[]{:S(2)}, u32[]{:S(2)}) collective-permute-start(bf16[512,1024]{1,0:T(8,128)(2,1)S(1)} %pad_maximum_fusion.5), channel_id=1, source_target_pairs={{0,2},{2,0},{4,6},{6,4},{1,3},{3,1},{5,7},{7,5},{8,10},{10,8},{12,... | collective-permute-start | bytes 3145736 | tf_op jit(solution)/shard_map/ppermute | solution.py:29
  28.2 5.8 %copy-start.10 = (bf16[512,1024]{1,0:T(8,128)(2,1)}, bf16[512,1024]{1,0:T(8,128)(2,1)S(1)}, u32[]{:S(2)}) copy-start(bf16[512,1024]{1,0:T(8,128)(2,1)S(1)} %collective-permute-done.12) | copy-start | bytes 3145732
  28.2 37.4 %collective-permute-start.14 = (bf16[512,1024]{1,0:T(8,128)(2,1)S(1)}, bf16[512,1024]{1,0:T(8,128)(2,1)}, u32[]{:S(2)}, u32[]{:S(2)}) collective-permute-start(bf16[512,1024]{1,0:T(8,128)(2,1)S(1)} %collective-permute-done.12), channel_id=1, source_target_pairs={{0,8},{8,0},{16,24},{24,16},{1,9},{9,1},{17,25},{25,17},{2,10},{10... | collective-permute-start | bytes 3145736 | tf_op jit(solution)/shard_map/ppermute | solution.py:29
  34.1 6.6 %copy-start = (bf16[1024,1024]{1,0:T(8,128)(2,1)S(1)}, bf16[1024,1024]{1,0:T(8,128)(2,1)}, u32[]{:S(2)}) copy-start(bf16[1024,1024]{1,0:T(8,128)(2,1)} %x_ref.7) | copy-start | bytes 6291460
  36.3 37.3 %collective-permute-start.2 = (bf16[2,64,1024]{2,1,0:T(8,128)(2,1)}, bf16[2,64,1024]{2,1,0:T(8,128)(2,1)}, u32[]{:S(2)}, u32[]{:S(2)}) collective-permute-start(bf16[2,64,1024]{2,1,0:T(8,128)(2,1)} %get-tuple-element.62), channel_id=1, source_target_pairs={{0,24},{8,16},{16,8},{24,0},{1,25},{9,17},{17,9},{25,1},{2,26},{10... | collective-permute-start | bytes 786440 | tf_op jit(solution)/shard_map/ppermute | solution.py:29
  38.8 34.9 %collective-permute-start.1 = (bf16[2,64,1024]{2,1,0:T(8,128)(2,1)}, bf16[2,64,1024]{2,1,0:T(8,128)(2,1)}, u32[]{:S(2)}, u32[]{:S(2)}) collective-permute-start(bf16[2,64,1024]{2,1,0:T(8,128)(2,1)} %get-tuple-element.63), channel_id=1, source_target_pairs={{0,16},{8,24},{16,0},{24,8},{1,17},{9,25},{17,1},{25,9},{2,18},{10... | collective-permute-start | bytes 786440 | tf_op jit(solution)/shard_map/ppermute | solution.py:29
  38.9 34.8 %collective-permute-start = (bf16[2,64,1024]{2,1,0:T(8,128)(2,1)}, bf16[2,64,1024]{2,1,0:T(8,128)(2,1)}, u32[]{:S(2)}, u32[]{:S(2)}) collective-permute-start(bf16[2,64,1024]{2,1,0:T(8,128)(2,1)} %get-tuple-element.64), channel_id=1, source_target_pairs={{0,8},{8,0},{16,24},{24,16},{1,9},{9,1},{17,25},{25,17},{2,10},{10... | collective-permute-start | bytes 786440 | tf_op jit(solution)/shard_map/ppermute | solution.py:29
  40.7 98.1 %collective-permute-start.23 = (bf16[1024,1024]{1,0:T(8,128)(2,1)S(1)}, bf16[1024,1024]{1,0:T(8,128)(2,1)}, u32[]{:S(2)}, u32[]{:S(2)}) collective-permute-start(bf16[1024,1024]{1,0:T(8,128)(2,1)S(1)} %copy-done), channel_id=1, source_target_pairs={{0,4},{2,6},{4,0},{6,2},{1,5},{3,7},{5,1},{7,3},{8,12},{10,14},{12... | collective-permute-start | bytes 6291464 | tf_op jit(solution)/shard_map/ppermute | solution.py:29
  69.0 66.6 %collective-permute-start.15 = (bf16[2,512,1024]{2,1,0:T(8,128)(2,1)}, bf16[2,512,1024]{2,1,0:T(8,128)(2,1)}, u32[]{:S(2)}, u32[]{:S(2)}) collective-permute-start(bf16[2,512,1024]{2,1,0:T(8,128)(2,1)} %pad_maximum_fusion), channel_id=1, source_target_pairs={{0,1},{1,0},{2,3},{3,2},{4,5},{5,4},{6,7},{7,6},{8,9},{9,8},{10,11... | collective-permute-start | bytes 6291464 | tf_op jit(solution)/shard_map/ppermute | solution.py:29
  81.7 10.1 %collective-permute-start.3 = (f32[256,64]{1,0:T(8,128)}, f32[256,64]{1,0:T(8,128)S(1)}, u32[]{:S(2)}, u32[]{:S(2)}) collective-permute-start(f32[256,64]{1,0:T(8,128)} %get-tuple-element.69), channel_id=1, source_target_pairs={{0,2},{2,0},{4,6},{6,4},{1,3},{3,1},{5,7},{7,5},{8,10},{10,8},{12,... | collective-permute-start | bytes 196616 | tf_op jit(solution)/shard_map/ppermute | solution.py:29
  83.5 8.5 %collective-permute-start.5 = (f32[256,64]{1,0:T(8,128)}, f32[256,64]{1,0:T(8,128)S(1)}, u32[]{:S(2)}, u32[]{:S(2)}) collective-permute-start(f32[256,64]{1,0:T(8,128)} %get-tuple-element.70), channel_id=1, source_target_pairs={{0,6},{2,4},{4,2},{6,0},{1,7},{3,5},{5,3},{7,1},{8,14},{10,12},{12... | collective-permute-start | bytes 196616 | tf_op jit(solution)/shard_map/ppermute | solution.py:29
  84.9 8.3 %collective-permute-start.4 = (f32[256,64]{1,0:T(8,128)S(1)}, f32[256,64]{1,0:T(8,128)}, u32[]{:S(2)}, u32[]{:S(2)}) collective-permute-start(f32[256,64]{1,0:T(8,128)S(1)} %get-tuple-element.71), channel_id=1, source_target_pairs={{0,4},{2,6},{4,0},{6,2},{1,5},{3,7},{5,1},{7,3},{8,12},{10,14},{12... | collective-permute-start | bytes 196616 | tf_op jit(solution)/shard_map/ppermute | solution.py:29
  94.3 5.8 %collective-permute-start.7 = (bf16[256,64]{1,0:T(8,128)(2,1)S(1)}, bf16[256,64]{1,0:T(8,128)(2,1)S(1)}, u32[]{:S(2)}, u32[]{:S(2)}) collective-permute-start(bf16[256,64]{1,0:T(8,128)(2,1)S(1)} %get-tuple-element.23), channel_id=1, source_target_pairs={{0,4},{2,6},{4,0},{6,2},{1,5},{3,7},{5,1},{7,3},{8,12},{10,14},{12... | collective-permute-start | bytes 98312 | tf_op jit(solution)/shard_map/ppermute | solution.py:29
  95.4 8.3 %collective-permute-start.6 = (bf16[256,64]{1,0:T(8,128)(2,1)S(1)}, bf16[256,64]{1,0:T(8,128)(2,1)S(1)}, u32[]{:S(2)}, u32[]{:S(2)}) collective-permute-start(bf16[256,64]{1,0:T(8,128)(2,1)S(1)} %get-tuple-element.23), channel_id=1, source_target_pairs={{0,2},{2,0},{4,6},{6,4},{1,3},{3,1},{5,7},{7,5},{8,10},{10,8},{12,... | collective-permute-start | bytes 98312 | tf_op jit(solution)/shard_map/ppermute | solution.py:29
  96.9 6.8 %collective-permute-start.8 = (bf16[256,64]{1,0:T(8,128)(2,1)S(1)}, bf16[256,64]{1,0:T(8,128)(2,1)S(1)}, u32[]{:S(2)}, u32[]{:S(2)}) collective-permute-start(bf16[256,64]{1,0:T(8,128)(2,1)S(1)} %get-tuple-element.23), channel_id=1, source_target_pairs={{0,6},{2,4},{4,2},{6,0},{1,7},{3,5},{5,3},{7,1},{8,14},{10,12},{12... | collective-permute-start | bytes 98312 | tf_op jit(solution)/shard_map/ppermute | solution.py:29
  100.1 11.4 %collective-permute-start.11 = (bf16[2,64,1024]{2,1,0:T(8,128)(2,1)}, bf16[2,64,1024]{2,1,0:T(8,128)(2,1)}, u32[]{:S(2)}, u32[]{:S(2)}) collective-permute-start(bf16[2,64,1024]{2,1,0:T(8,128)(2,1)} %get-tuple-element.59), channel_id=1, source_target_pairs={{0,24},{8,16},{16,8},{24,0},{1,25},{9,17},{17,9},{25,1},{2,26},{10... | collective-permute-start | bytes 786440 | tf_op jit(solution)/shard_map/ppermute | solution.py:29
  103.7 19.9 %collective-permute-start.10 = (bf16[2,64,1024]{2,1,0:T(8,128)(2,1)}, bf16[2,64,1024]{2,1,0:T(8,128)(2,1)}, u32[]{:S(2)}, u32[]{:S(2)}) collective-permute-start(bf16[2,64,1024]{2,1,0:T(8,128)(2,1)} %get-tuple-element.60), channel_id=1, source_target_pairs={{0,16},{8,24},{16,0},{24,8},{1,17},{9,25},{17,1},{25,9},{2,18},{10... | collective-permute-start | bytes 786440 | tf_op jit(solution)/shard_map/ppermute | solution.py:29
  103.7 19.9 %collective-permute-start.9 = (bf16[2,64,1024]{2,1,0:T(8,128)(2,1)}, bf16[2,64,1024]{2,1,0:T(8,128)(2,1)}, u32[]{:S(2)}, u32[]{:S(2)}) collective-permute-start(bf16[2,64,1024]{2,1,0:T(8,128)(2,1)} %get-tuple-element.61), channel_id=1, source_target_pairs={{0,8},{8,0},{16,24},{24,16},{1,9},{9,1},{17,25},{25,17},{2,10},{10... | collective-permute-start | bytes 786440 | tf_op jit(solution)/shard_map/ppermute | solution.py:29
  129.9 48.7 %collective-permute-start.13 = (bf16[1024,1024]{1,0:T(8,128)(2,1)}, bf16[1024,1024]{1,0:T(8,128)(2,1)S(1)}, u32[]{:S(2)}, u32[]{:S(2)}) collective-permute-start(bf16[1024,1024]{1,0:T(8,128)(2,1)} %x_ref.6), channel_id=1, source_target_pairs={{0,2},{2,0},{4,6},{6,4},{1,3},{3,1},{5,7},{7,5},{8,10},{10,8},{12,... | collective-permute-start | bytes 6291464 | tf_op jit(solution)/shard_map/ppermute | solution.py:29
  132.5 51.3 %collective-permute-start.17 = (f32[256,64]{1,0:T(8,128)S(1)}, f32[256,64]{1,0:T(8,128)S(1)}, u32[]{:S(2)}, u32[]{:S(2)}) collective-permute-start(f32[256,64]{1,0:T(8,128)S(1)} %get-tuple-element.66), channel_id=1, source_target_pairs={{0,2},{2,0},{4,6},{6,4},{1,3},{3,1},{5,7},{7,5},{8,10},{10,8},{12,... | collective-permute-start | bytes 196616 | tf_op jit(solution)/shard_map/ppermute | solution.py:29
  133.1 52.1 %collective-permute-start.19 = (f32[256,64]{1,0:T(8,128)S(1)}, f32[256,64]{1,0:T(8,128)S(1)}, u32[]{:S(2)}, u32[]{:S(2)}) collective-permute-start(f32[256,64]{1,0:T(8,128)S(1)} %get-tuple-element.67), channel_id=1, source_target_pairs={{0,6},{2,4},{4,2},{6,0},{1,7},{3,5},{5,3},{7,1},{8,14},{10,12},{12... | collective-permute-start | bytes 196616 | tf_op jit(solution)/shard_map/ppermute | solution.py:29
  135.5 49.7 %collective-permute-start.18 = (f32[256,64]{1,0:T(8,128)S(1)}, f32[256,64]{1,0:T(8,128)S(1)}, u32[]{:S(2)}, u32[]{:S(2)}) collective-permute-start(f32[256,64]{1,0:T(8,128)S(1)} %get-tuple-element.68), channel_id=1, source_target_pairs={{0,4},{2,6},{4,0},{6,2},{1,5},{3,7},{5,1},{7,3},{8,12},{10,14},{12... | collective-permute-start | bytes 196616 | tf_op jit(solution)/shard_map/ppermute | solution.py:29
  143.2 35.4 %copy-start.18 = (f32[1024,1024]{0,1:T(8,128)S(1)}, f32[1024,1024]{0,1:T(8,128)}, u32[]{:S(2)}) copy-start(f32[1024,1024]{0,1:T(8,128)} %fusion.10) | copy-start | bytes 12582916
  146.9 40.9 %copy-start.4 = (bf16[4,2,2,32,1024]{4,3,2,1,0:T(8,128)(2,1)S(1)}, bf16[4,2,2,32,1024]{4,3,2,1,0:T(8,128)(2,1)}, u32[]{:S(2)}) copy-start(bf16[4,2,2,32,1024]{4,3,2,1,0:T(8,128)(2,1)} %shard_map.101) | copy-start | bytes 3145732
  146.9 169.9 %collective-permute-start.24 = (bf16[1024,1024]{1,0:T(8,128)(2,1)}, bf16[1024,1024]{1,0:T(8,128)(2,1)S(1)}, u32[]{:S(2)}, u32[]{:S(2)}) collective-permute-start(bf16[1024,1024]{1,0:T(8,128)(2,1)} %fusion.1), channel_id=1, source_target_pairs={{0,2},{2,0},{4,6},{6,4},{1,3},{3,1},{5,7},{7,5},{8,10},{10,8},{12,... | collective-permute-start | bytes 6291464 | tf_op jit(solution)/shard_map/ppermute | solution.py:29
  182.3 138.9 %collective-permute-start.16 = (bf16[1024,1024]{1,0:T(8,128)(2,1)}, bf16[1024,1024]{1,0:T(8,128)(2,1)}, u32[]{:S(2)}, u32[]{:S(2)}) collective-permute-start(bf16[1024,1024]{1,0:T(8,128)(2,1)} %fusion), channel_id=1, source_target_pairs={{0,4},{2,6},{4,0},{6,2},{1,5},{3,7},{5,1},{7,3},{8,12},{10,14},{12... | collective-permute-start | bytes 6291464 | tf_op jit(solution)/shard_map/ppermute | solution.py:29
  186.2 41.4 %collective-permute-start.20 = (bf16[256,64]{1,0:T(8,128)(2,1)S(1)}, bf16[256,64]{1,0:T(8,128)(2,1)S(1)}, u32[]{:S(2)}, u32[]{:S(2)}) collective-permute-start(bf16[256,64]{1,0:T(8,128)(2,1)S(1)} %get-tuple-element.21), channel_id=1, source_target_pairs={{0,2},{2,0},{4,6},{6,4},{1,3},{3,1},{5,7},{7,5},{8,10},{10,8},{12,... | collective-permute-start | bytes 98312 | tf_op jit(solution)/shard_map/ppermute | solution.py:29
  188.7 53.4 %collective-permute-start.38 = (bf16[2,32,1024]{2,1,0:T(8,128)(2,1)}, bf16[2,32,1024]{2,1,0:T(8,128)(2,1)S(1)}, u32[]{:S(2)}, u32[]{:S(2)}) collective-permute-start(bf16[2,32,1024]{2,1,0:T(8,128)(2,1)} %get-tuple-element.42), channel_id=1, source_target_pairs={{0,25},{1,24},{8,17},{9,16},{16,9},{17,8},{24,1},{25,0},{2,27},{3,... | collective-permute-start | bytes 393224 | tf_op jit(solution)/shard_map/ppermute | solution.py:302
  188.7 53.5 %collective-permute-start.37 = (bf16[2,32,1024]{2,1,0:T(8,128)(2,1)}, bf16[2,32,1024]{2,1,0:T(8,128)(2,1)}, u32[]{:S(2)}, u32[]{:S(2)}) collective-permute-start(bf16[2,32,1024]{2,1,0:T(8,128)(2,1)} %get-tuple-element.43), channel_id=1, source_target_pairs={{0,24},{1,25},{8,16},{9,17},{16,8},{17,9},{24,0},{25,1},{2,26},{3,... | collective-permute-start | bytes 393224 | tf_op jit(solution)/shard_map/ppermute | solution.py:302
  227.6 4.3 %collective-permute-start.21 = (bf16[256,64]{1,0:T(8,128)(2,1)S(1)}, bf16[256,64]{1,0:T(8,128)(2,1)S(1)}, u32[]{:S(2)}, u32[]{:S(2)}) collective-permute-start(bf16[256,64]{1,0:T(8,128)(2,1)S(1)} %get-tuple-element.21), channel_id=1, source_target_pairs={{0,4},{2,6},{4,0},{6,2},{1,5},{3,7},{5,1},{7,3},{8,12},{10,14},{12... | collective-permute-start | bytes 98312 | tf_op jit(solution)/shard_map/ppermute | solution.py:29
  231.9 5.6 %collective-permute-start.22 = (bf16[256,64]{1,0:T(8,128)(2,1)S(1)}, bf16[256,64]{1,0:T(8,128)(2,1)S(1)}, u32[]{:S(2)}, u32[]{:S(2)}) collective-permute-start(bf16[256,64]{1,0:T(8,128)(2,1)S(1)} %get-tuple-element.21), channel_id=1, source_target_pairs={{0,6},{2,4},{4,2},{6,0},{1,7},{3,5},{5,3},{7,1},{8,14},{10,12},{12... | collective-permute-start | bytes 98312 | tf_op jit(solution)/shard_map/ppermute | solution.py:29
  237.6 9.5 %collective-permute-start.36 = (bf16[2,32,1024]{2,1,0:T(8,128)(2,1)}, bf16[2,32,1024]{2,1,0:T(8,128)(2,1)}, u32[]{:S(2)}, u32[]{:S(2)}) collective-permute-start(bf16[2,32,1024]{2,1,0:T(8,128)(2,1)} %get-tuple-element.44), channel_id=1, source_target_pairs={{0,17},{1,16},{8,25},{9,24},{16,1},{17,0},{24,9},{25,8},{2,19},{3,... | collective-permute-start | bytes 393224 | tf_op jit(solution)/shard_map/ppermute | solution.py:302
  242.1 4.9 %copy-start.15 = (bf16[2,32,1024]{2,1,0:T(8,128)(2,1)S(1)}, bf16[2,32,1024]{2,1,0:T(8,128)(2,1)}, u32[]{:S(2)}) copy-start(bf16[2,32,1024]{2,1,0:T(8,128)(2,1)} %get-tuple-element.47) | copy-start | bytes 393220
  242.1 9.8 %copy-start.14 = (bf16[2,32,1024]{2,1,0:T(8,128)(2,1)S(1)}, bf16[2,32,1024]{2,1,0:T(8,128)(2,1)}, u32[]{:S(2)}) copy-start(bf16[2,32,1024]{2,1,0:T(8,128)(2,1)} %get-tuple-element.48) | copy-start | bytes 393220
  242.1 35.8 %copy-start.11 = (bf16[2,32,1024]{2,1,0:T(8,128)(2,1)}, bf16[2,32,1024]{2,1,0:T(8,128)(2,1)S(1)}, u32[]{:S(2)}) copy-start(bf16[2,32,1024]{2,1,0:T(8,128)(2,1)S(1)} %collective-permute-done.38.refs_7_) | copy-start | bytes 393220
  242.2 9.8 %collective-permute-start.35 = (bf16[2,32,1024]{2,1,0:T(8,128)(2,1)}, bf16[2,32,1024]{2,1,0:T(8,128)(2,1)S(1)}, u32[]{:S(2)}, u32[]{:S(2)}) collective-permute-start(bf16[2,32,1024]{2,1,0:T(8,128)(2,1)} %get-tuple-element.45), channel_id=1, source_target_pairs={{0,16},{1,17},{8,24},{9,25},{16,0},{17,1},{24,8},{25,9},{2,18},{3,... | collective-permute-start | bytes 393224 | tf_op jit(solution)/shard_map/ppermute | solution.py:302
  242.2 9.7 %collective-permute-start.34 = (bf16[2,32,1024]{2,1,0:T(8,128)(2,1)}, bf16[2,32,1024]{2,1,0:T(8,128)(2,1)S(1)}, u32[]{:S(2)}, u32[]{:S(2)}) collective-permute-start(bf16[2,32,1024]{2,1,0:T(8,128)(2,1)} %get-tuple-element.46), channel_id=1, source_target_pairs={{0,9},{1,8},{8,1},{9,0},{16,25},{17,24},{24,17},{25,16},{2,11},{3,... | collective-permute-start | bytes 393224 | tf_op jit(solution)/shard_map/ppermute | solution.py:302
  247.1 7.8 %collective-permute-start.33 = (bf16[2,32,1024]{2,1,0:T(8,128)(2,1)S(1)}, bf16[2,32,1024]{2,1,0:T(8,128)(2,1)}, u32[]{:S(2)}, u32[]{:S(2)}) collective-permute-start(bf16[2,32,1024]{2,1,0:T(8,128)(2,1)S(1)} %copy-done.15), channel_id=1, source_target_pairs={{0,8},{1,9},{8,0},{9,1},{16,24},{17,25},{24,16},{25,17},{2,10},{3,... | collective-permute-start | bytes 393224 | tf_op jit(solution)/shard_map/ppermute | solution.py:302
  251.9 26.0 %copy-start.12 = (bf16[2,32,1024]{2,1,0:T(8,128)(2,1)}, bf16[2,32,1024]{2,1,0:T(8,128)(2,1)S(1)}, u32[]{:S(2)}) copy-start(bf16[2,32,1024]{2,1,0:T(8,128)(2,1)S(1)} %collective-permute-done.35.refs_4_) | copy-start | bytes 393220
  251.9 5.2 %collective-permute-start.32 = (bf16[2,32,1024]{2,1,0:T(8,128)(2,1)S(1)}, bf16[2,32,1024]{2,1,0:T(8,128)(2,1)}, u32[]{:S(2)}, u32[]{:S(2)}) collective-permute-start(bf16[2,32,1024]{2,1,0:T(8,128)(2,1)S(1)} %copy-done.14), channel_id=1, source_target_pairs={{0,1},{1,0},{8,9},{9,8},{16,17},{17,16},{24,25},{25,24},{2,3},{3,2... | collective-permute-start | bytes 393224 | tf_op jit(solution)/shard_map/ppermute | solution.py:302
  252.0 26.0 %copy-start.13 = (bf16[2,32,1024]{2,1,0:T(8,128)(2,1)}, bf16[2,32,1024]{2,1,0:T(8,128)(2,1)S(1)}, u32[]{:S(2)}) copy-start(bf16[2,32,1024]{2,1,0:T(8,128)(2,1)S(1)} %collective-permute-done.34.refs_3_) | copy-start | bytes 393220
  252.0 7.3 %collective-permute-start.31 = (bf16[2,32,1024]{2,1,0:T(8,128)(2,1)S(1)}, bf16[2,32,1024]{2,1,0:T(8,128)(2,1)}, u32[]{:S(2)}, u32[]{:S(2)}) collective-permute-start(bf16[2,32,1024]{2,1,0:T(8,128)(2,1)S(1)} %get-tuple-element.50), channel_id=1, source_target_pairs={{0,25},{1,24},{8,17},{9,16},{16,9},{17,8},{24,1},{25,0},{2,27},{3,... | collective-permute-start | bytes 393224 | tf_op jit(solution)/shard_map/ppermute | solution.py:302
  254.9 12.2 %collective-permute-start.30 = (bf16[2,32,1024]{2,1,0:T(8,128)(2,1)S(1)}, bf16[2,32,1024]{2,1,0:T(8,128)(2,1)}, u32[]{:S(2)}, u32[]{:S(2)}) collective-permute-start(bf16[2,32,1024]{2,1,0:T(8,128)(2,1)S(1)} %get-tuple-element.51), channel_id=1, source_target_pairs={{0,24},{1,25},{8,16},{9,17},{16,8},{17,9},{24,0},{25,1},{2,26},{3,... | collective-permute-start | bytes 393224 | tf_op jit(solution)/shard_map/ppermute | solution.py:302
  257.1 17.5 %collective-permute-start.29 = (bf16[2,32,1024]{2,1,0:T(8,128)(2,1)S(1)}, bf16[2,32,1024]{2,1,0:T(8,128)(2,1)}, u32[]{:S(2)}, u32[]{:S(2)}) collective-permute-start(bf16[2,32,1024]{2,1,0:T(8,128)(2,1)S(1)} %get-tuple-element.52), channel_id=1, source_target_pairs={{0,17},{1,16},{8,25},{9,24},{16,1},{17,0},{24,9},{25,8},{2,19},{3,... | collective-permute-start | bytes 393224 | tf_op jit(solution)/shard_map/ppermute | solution.py:302
  259.2 17.9 %collective-permute-start.28 = (bf16[2,32,1024]{2,1,0:T(8,128)(2,1)S(1)}, bf16[2,32,1024]{2,1,0:T(8,128)(2,1)}, u32[]{:S(2)}, u32[]{:S(2)}) collective-permute-start(bf16[2,32,1024]{2,1,0:T(8,128)(2,1)S(1)} %get-tuple-element.53), channel_id=1, source_target_pairs={{0,16},{1,17},{8,24},{9,25},{16,0},{17,1},{24,8},{25,9},{2,18},{3,... | collective-permute-start | bytes 393224 | tf_op jit(solution)/shard_map/ppermute | solution.py:302
  267.1 18.3 %collective-permute-start.27 = (bf16[2,32,1024]{2,1,0:T(8,128)(2,1)}, bf16[2,32,1024]{2,1,0:T(8,128)(2,1)}, u32[]{:S(2)}, u32[]{:S(2)}) collective-permute-start(bf16[2,32,1024]{2,1,0:T(8,128)(2,1)} %get-tuple-element.54), channel_id=1, source_target_pairs={{0,9},{1,8},{8,1},{9,0},{16,25},{17,24},{24,17},{25,16},{2,11},{3,... | collective-permute-start | bytes 393224 | tf_op jit(solution)/shard_map/ppermute | solution.py:302
  274.6 10.8 %collective-permute-start.26 = (bf16[2,32,1024]{2,1,0:T(8,128)(2,1)}, bf16[2,32,1024]{2,1,0:T(8,128)(2,1)}, u32[]{:S(2)}, u32[]{:S(2)}) collective-permute-start(bf16[2,32,1024]{2,1,0:T(8,128)(2,1)} %get-tuple-element.55), channel_id=1, source_target_pairs={{0,8},{1,9},{8,0},{9,1},{16,24},{17,25},{24,16},{25,17},{2,10},{3,... | collective-permute-start | bytes 393224 | tf_op jit(solution)/shard_map/ppermute | solution.py:302
  277.1 8.3 %collective-permute-start.25 = (bf16[2,32,1024]{2,1,0:T(8,128)(2,1)}, bf16[2,32,1024]{2,1,0:T(8,128)(2,1)}, u32[]{:S(2)}, u32[]{:S(2)}) collective-permute-start(bf16[2,32,1024]{2,1,0:T(8,128)(2,1)} %get-tuple-element.56), channel_id=1, source_target_pairs={{0,1},{1,0},{8,9},{9,8},{16,17},{17,16},{24,25},{25,24},{2,3},{3,2... | collective-permute-start | bytes 393224 | tf_op jit(solution)/shard_map/ppermute | solution.py:302
  (10 other events, 29.6 us)
